TPU v7x, 256 devices: a whole 4x4x8 slice. The times are simulated.
256 devices in a mesh: expert: 8 (over y, core), tensor: 32 (over z, x).
Axes of the slice: x: 4, y: 4, z: 8, core: 2. Of those that a mesh axis runs over, the one named last changes fastest.
Arguments:
- tokens: bfloat16 [2048, 6144], P('expert', 'tensor'), may hold values from -6 to 6
- expert_ids: int32 [2048, 2], P('expert'), may hold values from 0 to 7, all different within a row; in each aligned block of 256 rows (0 to 255, 256 to 511, ...) at most 96 rows name the same one
- gate_prob: float32 [2048, 2], P('expert'), may hold values from 0.1 to 1
- w_gate: bfloat16 [8, 6144, 8192], P('expert', None, 'tensor'), may hold values from -0.078125 to 0.078125
- w_up: bfloat16 [8, 6144, 8192], P('expert', None, 'tensor'), may hold values from -0.078125 to 0.078125
- w_down: bfloat16 [8, 8192, 6144], P('expert', 'tensor'), may hold values from -0.125 to 0.125
Outputs:
- mixed: bfloat16 [2048, 6144], P('expert', 'tensor')
Inputs may be any that keep to these rules, and one draw needn't show every extreme that they name: `expert_ids`: the two experts of a row differ. Within the rows of one index of expert (aligned blocks of 256 rows) no expert is named by more than 96 rows, and in every draw some expert is named by exactly 96 rows of some block.
All inputs are finite; a program needn't handle non-finite values.
Results may differ from a plain program's by a relative error of at most 0.017.
Values may be sent and summed in bfloat16 or wider, within the bound.
No kernel may reach another device: no remote copies, remote signals or barrier semaphores. Data moves between devices by JAX's collectives and lax.ppermute only.
A program may use at most 64 MiB of HBM per device.

v0:
```python
import jax
import jax.numpy as jnp
from jax import lax
from jax.sharding import PartitionSpec as P


def slot_table(ids, experts, cap):
    flat = ids.reshape(-1)
    onehot = (flat[:, None] == jnp.arange(experts, dtype=jnp.int32)[None, :]).astype(jnp.int32)
    before = jnp.cumsum(onehot, axis=0) - onehot
    position = jnp.sum(before * onehot, axis=1)
    slot = flat * cap + position
    match = slot[None, :] == jnp.arange(experts * cap, dtype=jnp.int32)[:, None]
    which = jnp.arange(flat.shape[0], dtype=jnp.int32) // 2
    owner = jnp.max(jnp.where(match, which[None, :], -1), axis=1)
    return (slot, owner)


def fill_slots(block, owner):
    picked = jnp.take(block, jnp.maximum(owner, 0), axis=0)
    return jnp.where((owner >= 0)[:, None], picked, jnp.zeros_like(picked))


def local(tokens, expert_ids, gate_prob, w_gate, w_up, w_down):
    experts = lax.axis_size("expert")
    group_rows = tokens.shape[0]
    cap = 3 * group_rows // experts
    slot, owner = slot_table(expert_ids, experts, cap)
    gate_mat = w_gate[0]
    up_mat = w_up[0]
    down_mat = w_down[0]
    columns = tokens.shape[1]
    sending = fill_slots(tokens, owner).reshape(experts, cap, columns)
    arrived = lax.all_to_all(sending, "expert", split_axis=0, concat_axis=0, tiled=True).reshape(
        experts * cap, columns
    )
    piece = lax.all_gather(arrived, "tensor", axis=1, tiled=True)
    gate = jnp.dot(piece, gate_mat, preferred_element_type=jnp.float32)
    up = jnp.dot(piece, up_mat, preferred_element_type=jnp.float32)
    hidden = (jax.nn.silu(gate) * up).astype(jnp.bfloat16)
    partial_out = jnp.dot(hidden, down_mat, preferred_element_type=jnp.float32)
    summed = lax.psum_scatter(
        partial_out.astype(jnp.bfloat16), "tensor", scatter_dimension=1, tiled=True
    ).astype(jnp.float32)
    columns = summed.shape[1]
    returned = lax.all_to_all(
        summed.reshape(experts, cap, columns).astype(jnp.bfloat16),
        "expert",
        split_axis=0,
        concat_axis=0,
        tiled=True,
    ).astype(jnp.float32)
    table = returned.reshape(experts * cap, columns)
    picked = jnp.take(table, slot, axis=0).reshape(group_rows, 2, columns)
    mixed = jnp.sum(gate_prob[:, :, None] * picked, axis=1)
    return mixed.astype(jnp.bfloat16)


def solution(mesh):
    return jax.shard_map(
        local,
        mesh=mesh,
        in_specs=(
            P("expert", "tensor"),
            P("expert", None),
            P("expert", None),
            P("expert", None, "tensor"),
            P("expert", None, "tensor"),
            P("expert", "tensor", None),
        ),
        out_specs=P("expert", "tensor"),
        check_vma=False,
    )
```

profile of v0, /device:TPU:1, one launch (start us, length us, event | category | flops | bytes accessed | tf_op | source)
XLA Modules:
  0.0 413.5 jit_solution(16867759176059031204)
XLA Ops:
  6.5 1.0 copy.36
  7.5 0.1 eq.39
  7.7 0.1 reshape.131
  7.8 1.1 reduce-window.6
  9.0 0.2 slice_reduce_fusion
  9.3 0.3 select_reduce_fusion
  9.8 1.0 copy.40
  10.8 3.3 gather_fusion
  14.1 1.3 select_select_fusion
  15.4 13.8 %all_to_all.10 = bf16[8,96,192]{2,1,0:T(8,128)(2,1)S(1)} all-to-all(bf16[8,96,192]{2,1,0:T(8,128)(2,1)S(1)} %select_select_fusion), channel_id=1, replica_groups=mesh['expert'=8,'tensor'=32] {'expert'}, dimensions={0} | all-to-all | bytes 589824 | tf_op jit(solution)/shard_map/all_to_all | solution.py:34
  29.2 0.9 copy.46
  30.1 103.6 %all-gather.2.cloned.1.call-done = bf16[768,6144]{0,1:T(8,128)(2,1)} async-done(((bf16[768,192]{0,1:T(8,128)(2,1)}), bf16[768,6144]{0,1:T(8,128)(2,1)}) %all-gather.2.cloned.1.call-update) | async-done | bytes 9437200 | tf_op jit(solution)/shard_map/all_gather | solution.py:37
  133.7 6.3 %fusion.3 = f32[768,256]{1,0:T(8,128)S(1)} fusion(bf16[768,6144]{0,1:T(8,128)(2,1)} %all-gather.2.cloned.1.call-done, bf16[1,6144,256]{2,1,0:T(8,128)(2,1)} %param.9), kind=kOutput, calls=%fused_computation.6 | convolution fusion | flops 2415919104 | bytes 13369344 | tf_op jit(solution)/shard_map/dot_general | solution.py:38
  140.1 1.0 copy-done.1
  141.1 0.9 copy-done.6
  142.0 2.7 fusion.8
  144.6 5.1 %convolution_convert_fusion = bf16[768,6144]{0,1:T(8,128)(2,1)} fusion(bf16[768,256]{1,0:T(8,128)(2,1)S(1)} %fusion.8, bf16[1,256,6144]{2,1,0:T(8,128)(2,1)S(1)} %copy-done), kind=kOutput, calls=%fused_computation.2 | convolution fusion | flops 2420637696 | bytes 12976128 | tf_op jit(solution)/shard_map/dot_general | solution.py:41
  149.8 0.1 reduce_sum.23
  149.9 0.5 copy-done.4
  150.6 0.1 mul.53
  150.8 0.8 copy.39
  151.6 0.8 copy.35
  152.4 225.5 %reduce-scatter.2.cloned.1.call-done = bf16[768,192]{0,1:T(8,128)(2,1)} async-done(((bf16[768,6144]{0,1:T(8,128)(2,1)}), bf16[768,192]{0,1:T(8,128)(2,1)}) %reduce-scatter.2.cloned.1.call-update) | async-done | bytes 294928 | tf_op jit(solution)/shard_map/reduce_scatter | solution.py:42
  377.9 1.4 convert_element_type.26
  379.3 0.8 copy.42
  380.1 9.0 %all-to-all-start.1 = ((bf16[8,96,192]{1,2,0:T(8,128)(2,1)}), bf16[8,96,192]{1,2,0:T(8,128)(2,1)S(1)}, u32[]{:S(2)}, u32[]{:S(2)}) async-start(bf16[8,96,192]{1,2,0:T(8,128)(2,1)} %copy.42), calls=%async_computation.2 | async-start | bytes 786432 | tf_op jit(solution)/shard_map/all_to_all | solution.py:46
  389.2 7.7 %all-to-all-done.1 = bf16[8,96,192]{1,2,0:T(8,128)(2,1)S(1)} async-done(((bf16[8,96,192]{1,2,0:T(8,128)(2,1)}), bf16[8,96,192]{1,2,0:T(8,128)(2,1)S(1)}, u32[]{:S(2)}, u32[]{:S(2)}) %all-to-all-start.1) | async-done | bytes 294944 | tf_op jit(solution)/shard_map/all_to_all | solution.py:46
  396.8 1.1 copy.43
  397.9 3.4 gather_fusion.1
  401.3 2.1 gather.15
  403.5 2.4 multiply_reduce_fusion
  405.9 0.7 copy.45
  (31 shorter events, 0.7 us)
Async XLA Ops:
  6.5 138.1 %copy-start = (bf16[1,256,6144]{2,1,0:T(8,128)(2,1)S(1)}, bf16[1,256,6144]{2,1,0:T(8,128)(2,1)}, u32[]{:S(2)}) copy-start(bf16[1,256,6144]{2,1,0:T(8,128)(2,1)} %param.11) | copy-start | bytes 9437188
  6.5 127.2 %all-gather.2.cloned.1.call-start = ((), (), s32[]{:S(2)}) async-start(), calls=%async_computation.3 | async-start | bytes 9732096 | tf_op jit(solution)/shard_map/all_gather | solution.py:37
  30.1 347.9 %reduce-scatter.2.cloned.1.call-start = ((), (), s32[]{:S(2)}) async-start(), calls=%async_computation.4 | async-start | bytes 9732096 | tf_op jit(solution)/shard_map/reduce_scatter | solution.py:42
  133.7 7.3 %copy-start.1 = (bf16[768,6144]{0,1:T(8,128)(2,1)S(1)}, bf16[768,6144]{0,1:T(8,128)(2,1)}, u32[]{:S(2)}) copy-start(bf16[768,6144]{0,1:T(8,128)(2,1)} %all-gather.2.cloned.1.call-done) | copy-start | bytes 28311556
  133.7 8.2 %copy-start.6 = (bf16[1,6144,256]{2,1,0:T(8,128)(2,1)S(1)}, bf16[1,6144,256]{2,1,0:T(8,128)(2,1)}, u32[]{:S(2)}) copy-start(bf16[1,6144,256]{2,1,0:T(8,128)(2,1)} %param.10) | copy-start | bytes 9437188
  149.7 0.7 copy-start.4
  149.7 1.9 copy-start.5
  380.1 16.7 %all-to-all-start.1 = ((bf16[8,96,192]{1,2,0:T(8,128)(2,1)}), bf16[8,96,192]{1,2,0:T(8,128)(2,1)S(1)}, u32[]{:S(2)}, u32[]{:S(2)}) async-start(bf16[8,96,192]{1,2,0:T(8,128)(2,1)} %copy.42), calls=%async_computation.2 | async-start | bytes 786432 | tf_op jit(solution)/shard_map/all_to_all | solution.py:46
  397.9 5.6 %copy-start.2 = (f32[256,2]{1,0:T(8,128)S(1)}, f32[256,2]{1,0:T(8,128)}, u32[]{:S(2)}) copy-start(f32[256,2]{1,0:T(8,128)} %copy.35) | copy-start | bytes 6148
  397.9 5.6 %copy-start.3 = (pred[256,2]{1,0:T(8,128)(4,1)S(1)}, pred[256,2]{1,0:T(8,128)(4,1)}, u32[]{:S(2)}) copy-start(pred[256,2]{1,0:T(8,128)(4,1)} %copy.39) | copy-start | bytes 1540
Sparse Core Ops, SparseCore 0:
  30.2 103.4 all-gather.1
  149.9 228.0 reduce-scatter.1
where the time goes:
time: 414 us
  waiting for transfers between devices  337 us (81%)
  local copies, waits for them, and re-layouts  20.9 us (5%)
  matrix products  14.1 us (3%)
  blocking collectives  13.8 us (3%)
  between operations  13.6 us (3%)
  starting transfers between devices  9.05 us (2%)
  other arithmetic  5.31 us (1%)
    reduce_scatter x1, waiting for transfers between devices, local(): lax.psum_scatter(partial_out.astype(jnp.bfloat16), 'tensor', scatter_dime...  226 us
    all_gather x1, waiting for transfers between devices, local(): piece = lax.all_gather(arrived, 'tensor', axis=1, tiled=True)  104 us
    all_to_all x1, blocking collectives, local(): lax.all_to_all(sending, 'expert', split_axis=0, concat_axis=0, tiled=True)  13.8 us
    all_to_all x1, starting transfers between devices, local(): lax.all_to_all(summed.reshape(experts, cap, columns).astype(jnp.bfloat16)...  9 us
  transfers between devices with their start and end apart: 3, of which 3 were waited for; matrix products, arithmetic and copies ran while one was open for 1% of the time, Pallas kernels for 0%

commit v1 on v0

v1 whole, which is shorter than its diff:
```python
import jax
import jax.numpy as jnp
from jax import lax
from jax.sharding import Mesh
from jax.sharding import PartitionSpec as P

NZ = 8
NX = 4


def ring(n, d):
    return [(i, (i + d) % n) for i in range(n)]


def slot_onehots(ids, experts, cap):
    rows = ids.shape[0]
    lanes = jnp.arange(experts, dtype=jnp.int32)[None, :]
    first = ids[:, 0:1] == lanes
    second = ids[:, 1:2] == lanes
    named = (first | second).astype(jnp.bfloat16)
    i = jnp.arange(rows, dtype=jnp.int32)
    lower = (i[:, None] > i[None, :]).astype(jnp.bfloat16)
    before = jnp.dot(lower, named, preferred_element_type=jnp.float32).astype(jnp.int32)
    position = jnp.arange(cap, dtype=jnp.int32)[None, None, :]
    hit = before[:, :, None] == position
    return first, second, hit


def local(tokens, expert_ids, gate_prob, w_gate, w_up, w_down):
    experts = 8
    rows, columns = tokens.shape
    cap = 3 * rows // experts
    slots = experts * cap
    width = w_gate.shape[2]
    model = w_gate.shape[1]
    first, second, hit = slot_onehots(expert_ids, experts, cap)
    pick = (hit & (first | second)[:, :, None]).astype(jnp.bfloat16).reshape(rows, slots)
    weight = (
        jnp.where(first, gate_prob[:, 0:1], 0.0) + jnp.where(second, gate_prob[:, 1:2], 0.0)
    )
    mix = jnp.where(hit, weight[:, :, None], 0.0).reshape(rows, slots)

    sending = jnp.dot(tokens.T, pick, preferred_element_type=jnp.float32).astype(jnp.bfloat16)
    sending = sending.reshape(columns, experts, cap).transpose(1, 0, 2)
    arrived = lax.all_to_all(sending, ("y", "c"), split_axis=0, concat_axis=0, tiled=True)
    arrived = arrived.transpose(1, 0, 2).reshape(columns, slots)
    piece = lax.all_gather(arrived, ("z", "x"), axis=0, tiled=True)

    down, _ = lax.optimization_barrier((w_down[0], arrived))
    down = down.reshape(width, NZ, NX, columns).transpose(2, 0, 1, 3).reshape(NX, width, NZ * columns)
    down = lax.all_to_all(down, "x", split_axis=0, concat_axis=0, tiled=True)
    me = lax.axis_index("x")
    downs = [
        lax.dynamic_slice(
            down, ((me + k) & (NX - 1), 0, 0), (1,) + down.shape[1:], allow_negative_indices=False
        )[0]
        for k in range(NX)
    ]

    contract = (((0,), (0,)), ((), ()))
    gate = lax.dot_general(w_gate[0], piece, contract, preferred_element_type=jnp.float32)
    up = lax.dot_general(w_up[0], piece, contract, preferred_element_type=jnp.float32)
    hidden = (jax.nn.silu(gate) * up).astype(jnp.bfloat16)
    half = slots // 2
    from_left = lax.ppermute(hidden, "x", ring(NX, 1))
    from_right = lax.ppermute(hidden, "x", ring(NX, -1))
    far_top = lax.ppermute(from_left[:, :half], "x", ring(NX, 1))
    far_bottom = lax.ppermute(from_right[:, half:], "x", ring(NX, -1))
    far = jnp.concatenate([far_top, far_bottom], axis=1)
    part = lax.dot_general(downs[0], hidden, contract, preferred_element_type=jnp.float32)
    part += lax.dot_general(downs[3], from_left, contract, preferred_element_type=jnp.float32)
    part += lax.dot_general(downs[1], from_right, contract, preferred_element_type=jnp.float32)
    part += lax.dot_general(downs[2], far, contract, preferred_element_type=jnp.float32)
    summed = lax.psum_scatter(part.astype(jnp.bfloat16), "z", scatter_dimension=0, tiled=True)

    back = summed.reshape(columns, experts, cap).transpose(1, 0, 2)
    back = lax.all_to_all(back, ("y", "c"), split_axis=0, concat_axis=0, tiled=True)
    table = back.transpose(1, 0, 2).reshape(columns, slots)
    high = lax.reduce_precision(mix, 8, 7)
    low = (mix - high).astype(jnp.bfloat16)
    high = high.astype(jnp.bfloat16)
    last = (((1,), (1,)), ((), ()))
    mixed = lax.dot_general(table, high, last, preferred_element_type=jnp.float32)
    mixed += lax.dot_general(table, low, last, preferred_element_type=jnp.float32)
    return mixed.astype(jnp.bfloat16).T


def solution(mesh):
    grid = Mesh(mesh.devices.reshape(4, 2, NZ, NX), ("y", "c", "z", "x"))
    group = ("y", "c")
    tensor = ("z", "x")
    return jax.shard_map(
        local,
        mesh=grid,
        in_specs=(
            P(group, tensor),
            P(group, None),
            P(group, None),
            P(group, None, tensor),
            P(group, None, tensor),
            P(group, tensor, None),
        ),
        out_specs=P(group, tensor),
        check_vma=False,
    )
```

time: 414 us -> 234 us (0.57)
  waiting for transfers between devices: 337 us -> 144 us
  starting transfers between devices: 9.05 us -> 19.3 us
  matrix products: 14.1 us -> 23.1 us
  other arithmetic: 5.31 us -> 0.84 us
    reduce_scatter x1, waiting for transfers between devices: 226 us -> 38.5 us  [local(): lax.psum_scatter(part.astype(jnp.bfloat16), 'z', scatter_dimension=0, til...]
    all_gather x1, waiting for transfers between devices: 104 us -> 92.8 us  [local(): piece = lax.all_gather(arrived, ('z', 'x'), axis=0, tiled=True)]
    dot_general x3 -> x10, matrix products: 14.1 us -> 23.1 us  [the longest x1 5.35 us: local(): lax.dot_general(w_gate[0], piece, contract, preferred_element_type=jnp.fl...]
    gather x3 -> x0, local copies, waits for them, and re-layouts: 8.83 us -> none  [the longest x2 5.55 us: local(): picked = jnp.take(table, slot, axis=0).reshape(group_rows, 2, columns)]
    ppermute x0 -> x4, waiting for transfers between devices: none -> 6.37 us  [the longest x1 6.36 us: local(): from_left = lax.ppermute(hidden, 'x', ring(NX, 1))]
    ppermute x0 -> x4, starting transfers between devices: none -> 5.67 us  [the longest x1 2.91 us: local(): far_bottom = lax.ppermute(from_right[:, half:], 'x', ring(NX, -1))]
    all_to_all x1 -> x2, starting transfers between devices: 9 us -> 13.6 us  [the longest x1 8.98 us: local(): lax.all_to_all(back, ('y', 'c'), split_axis=0, concat_axis=0, tiled=True)]
  transfers between devices with their start and end apart: 3 -> 8, of which waited for: 3 -> 4; matrix products, arithmetic and copies ran while one was open for 1% -> 11% of each run, Pallas kernels for 0% -> 0%
where the time goes in v1:
time: 234 us; the launch traced here: 233 us
  waiting for transfers between devices  144 us (62%)
  matrix products  23.1 us (10%)
  starting transfers between devices  19.3 us (8%)
  local copies, waits for them, and re-layouts  18.1 us (8%)
  blocking collectives  13.8 us (6%)
  between operations  13.5 us (6%)
    all_gather x1, waiting for transfers between devices, local(): piece = lax.all_gather(arrived, ('z', 'x'), axis=0, tiled=True)  92.8 us
    reduce_scatter x1, waiting for transfers between devices, local(): lax.psum_scatter(part.astype(jnp.bfloat16), 'z', scatter_dimension=0, til...  38.5 us
    all_to_all x1, blocking collectives, local(): lax.all_to_all(sending, ('y', 'c'), split_axis=0, concat_axis=0, tiled=True)  13.8 us
    all_to_all x1, starting transfers between devices, local(): lax.all_to_all(back, ('y', 'c'), split_axis=0, concat_axis=0, tiled=True)  8.98 us
    unnamed x7, local copies, waits for them, and re-layouts  6.64 us
    ppermute x1, waiting for transfers between devices, local(): from_left = lax.ppermute(hidden, 'x', ring(NX, 1))  6.36 us
    all_to_all x1, waiting for transfers between devices, local(): lax.all_to_all(back, ('y', 'c'), split_axis=0, concat_axis=0, tiled=True)  6.34 us
    dot_general x1, matrix products, local(): lax.dot_general(w_gate[0], piece, contract, preferred_element_type=jnp.fl...  5.35 us
  transfers between devices with their start and end apart: 8, of which 4 were waited for; matrix products, arithmetic and copies ran while one was open for 11% of the time, Pallas kernels for 0%

profile of v1, /device:TPU:1, one launch (start us, length us, event | category | flops | bytes accessed | tf_op | source)
XLA Modules:
  0.0 232.8 jit_solution(7611654917233498801)
XLA Ops:
  6.5 0.9 fusion.57
  7.9 1.9 fusion.16
  9.8 1.4 reshape.157
  11.3 13.8 %all_to_all.15 = bf16[8,192,96]{2,1,0:T(8,128)(2,1)S(1)} all-to-all(bf16[8,192,96]{2,1,0:T(8,128)(2,1)S(1)} %bitcast.82), channel_id=1, replica_groups=mesh['y'=4,'c'=2,'z'=8,'x'=4] {'y','c'}, dimensions={0} | all-to-all | bytes 589824 | tf_op jit(solution)/shard_map/all_to_all | solution.py:45
  25.1 0.3 copy.17
  25.3 1.0 reshape.158
  26.4 4.7 %copy.15 = bf16[1,256,6144]{1,2,0:T(8,128)(2,1)} copy(bf16[1,256,6144]{2,1,0:T(8,128)(2,1)} %param.11) | data formatting | bytes 6291456 | tf_op args[5]
  31.1 3.9 %copy.18 = bf16[4,256,8,192]{1,3,2,0:T(8,128)(2,1)} copy(bf16[4,256,8,192]{1,3,0,2:T(8,128)(2,1)} %bitcast.81) | data formatting | bytes 6291456 | tf_op jit(solution)/shard_map/transpose | solution.py:50
  34.9 4.7 %all-to-all-start.1 = ((bf16[4,256,1536]{1,2,0:T(8,128)(2,1)}), bf16[4,256,1536]{1,2,0:T(8,128)(2,1)}, u32[]{:S(2)}, u32[]{:S(2)}) async-start(bf16[4,256,1536]{1,2,0:T(8,128)(2,1)} %bitcast.80), calls=%async_computation.1 | async-start | bytes 6291456 | tf_op jit(solution)/shard_map/all_to_all | solution.py:51
  39.6 92.8 %all-gather.2.cloned.1.call-done = bf16[6144,768]{1,0:T(8,128)(2,1)} async-done(((bf16[192,768]{1,0:T(8,128)(2,1)}), bf16[6144,768]{1,0:T(8,128)(2,1)}) %all-gather.2.cloned.1.call-update) | async-done | bytes 9437200 | tf_op jit(solution)/shard_map/all_gather | solution.py:47
  132.4 5.3 %fusion.4 = f32[256,768]{0,1:T(8,128)S(1)} fusion(bf16[6144,768]{1,0:T(8,128)(2,1)} %all-gather.2.cloned.1.call-done, bf16[1,6144,256]{2,1,0:T(8,128)(2,1)S(1)} %copy-done), kind=kOutput, calls=%fused_computation.5 | convolution fusion | flops 2415919104 | bytes 13369344 | tf_op jit(solution)/shard_map/dot_general | solution.py:61
  137.7 1.1 copy-done.1
  138.8 0.9 copy-done.2
  139.7 3.4 %fusion.13 = bf16[256,768]{0,1:T(8,128)(2,1)} fusion(bf16[6144,768]{1,0:T(8,128)(2,1)S(1)} %copy-done.1, bf16[1,6144,256]{2,1,0:T(8,128)(2,1)S(1)} %copy-done.2, f32[256,768]{0,1:T(8,128)S(1)} %fusion.4), kind=kOutput, calls=%fused_computation.8 | convolution fusion | flops 2417098752 | bytes 13762560 | tf_op jit(solution)/shard_map/dot_general | solution.py:62
  143.2 0.3 collective-permute-start
  143.4 2.4 %collective-permute-start.1 = (bf16[256,768]{0,1:T(8,128)(2,1)}, bf16[256,768]{0,1:T(8,128)(2,1)}, u32[]{:S(2)}, u32[]{:S(2)}) collective-permute-start(bf16[256,768]{0,1:T(8,128)(2,1)} %fusion.13), channel_id=1, source_target_pairs={{0,3},{1,0},{2,1},{3,2},{4,7},{5,4},{6,5},{7,6},{8,11},{9,8},{10,9... | collective-permute-start | bytes 1179656 | tf_op jit(solution)/shard_map/ppermute | solution.py:66
  145.8 2.0 fusion.28
  147.9 6.4 %collective-permute-done = bf16[256,768]{0,1:T(8,128)(2,1)S(1)} collective-permute-done((bf16[256,768]{0,1:T(8,128)(2,1)}, bf16[256,768]{0,1:T(8,128)(2,1)S(1)}, u32[]{:S(2)}, u32[]{:S(2)}) %collective-permute-start) | collective-permute-done | bytes 393248 | tf_op jit(solution)/shard_map/ppermute | solution.py:65
  154.4 0.9 slice.31
  155.3 2.9 %collective-permute-start.3 = (bf16[256,384]{0,1:T(8,128)(2,1)S(1)}, bf16[256,384]{0,1:T(8,128)(2,1)S(1)}, u32[]{:S(2)}, u32[]{:S(2)}) collective-permute-start(bf16[256,384]{0,1:T(8,128)(2,1)S(1)} %slice.31), channel_id=1, source_target_pairs={{0,3},{1,0},{2,1},{3,2},{4,7},{5,4},{6,5},{7,6},{8,11},{9,8},{10,9... | collective-permute-start | bytes 589832 | tf_op jit(solution)/shard_map/ppermute | solution.py:68
  158.2 1.9 fusion.26
  160.2 2.0 fusion.24
  162.2 3.6 %add_convert_fusion = bf16[1536,768]{1,0:T(8,128)(2,1)} fusion(f32[1536,768]{1,0:T(8,128)S(1)} %fusion.24, f32[1536,768]{1,0:T(8,128)S(1)} %fusion.28, f32[1536,768]{1,0:T(8,128)S(1)} %fusion.26, bf16[4,256,1536]{1,2,0:T(8,128)(2,1)} %all-to-all-done.1, s32[]{:T(128)S(6)} %and.30, bf16[256,384]{0,1:T(8,128)(2,1)S(1)} %collective-permute-done.3, ...), kind=kOutput, calls=%fused_computation | convolution fusion | flops 609484800 | bytes 17694724 | tf_op jit(solution)/shard_map/dot_general | solution.py:73
  165.8 38.5 %reduce-scatter.2.cloned.1.call-done = bf16[192,768]{1,0:T(8,128)(2,1)} async-done(((bf16[1536,768]{1,0:T(8,128)(2,1)}), bf16[192,768]{1,0:T(8,128)(2,1)}) %reduce-scatter.2.cloned.1.call-update) | async-done | bytes 294928 | tf_op jit(solution)/shard_map/reduce_scatter | solution.py:74
  204.4 1.4 reshape.161
  205.8 0.8 copy.22
  206.6 9.0 %all-to-all-start.2 = ((bf16[8,192,96]{2,1,0:T(8,128)(2,1)}), bf16[8,192,96]{2,1,0:T(8,128)(2,1)S(1)}, u32[]{:S(2)}, u32[]{:S(2)}) async-start(bf16[8,192,96]{2,1,0:T(8,128)(2,1)} %bitcast.78), calls=%async_computation.3 | async-start | bytes 786432 | tf_op jit(solution)/shard_map/all_to_all | solution.py:77
  215.6 0.8 fusion.56
  216.3 0.6 select_add_fusion
  216.9 6.3 %all-to-all-done.2 = bf16[8,192,96]{2,1,0:T(8,128)(2,1)S(1)} async-done(((bf16[8,192,96]{2,1,0:T(8,128)(2,1)}), bf16[8,192,96]{2,1,0:T(8,128)(2,1)S(1)}, u32[]{:S(2)}, u32[]{:S(2)}) %all-to-all-start.2) | async-done | bytes 294944 | tf_op jit(solution)/shard_map/all_to_all | solution.py:77
  223.3 1.0 convolution_bitcast_fusion
  224.3 1.6 fusion.18
  (20 shorter events, 0.7 us)
Async XLA Ops:
  6.5 125.8 %copy-start = (bf16[1,6144,256]{2,1,0:T(8,128)(2,1)S(1)}, bf16[1,6144,256]{2,1,0:T(8,128)(2,1)}, u32[]{:S(2)}) copy-start(bf16[1,6144,256]{2,1,0:T(8,128)(2,1)} %param.9) | copy-start | bytes 9437188
  6.5 125.8 %all-gather.2.cloned.1.call-start = ((), (), s32[]{:S(2)}) async-start(), calls=%async_computation.4 | async-start | bytes 9732096 | tf_op jit(solution)/shard_map/all_gather | solution.py:47
  34.9 110.9 %all-to-all-start.1 = ((bf16[4,256,1536]{1,2,0:T(8,128)(2,1)}), bf16[4,256,1536]{1,2,0:T(8,128)(2,1)}, u32[]{:S(2)}, u32[]{:S(2)}) async-start(bf16[4,256,1536]{1,2,0:T(8,128)(2,1)} %bitcast.80), calls=%async_computation.1 | async-start | bytes 6291456 | tf_op jit(solution)/shard_map/all_to_all | solution.py:51
  39.6 164.8 %reduce-scatter.2.cloned.1.call-start = ((), (), s32[]{:S(2)}) async-start(), calls=%async_computation.5 | async-start | bytes 2654208 | tf_op jit(solution)/shard_map/reduce_scatter | solution.py:74
  132.4 6.4 %copy-start.1 = (bf16[6144,768]{1,0:T(8,128)(2,1)S(1)}, bf16[6144,768]{1,0:T(8,128)(2,1)}, u32[]{:S(2)}) copy-start(bf16[6144,768]{1,0:T(8,128)(2,1)} %all-gather.2.cloned.1.call-done) | copy-start | bytes 28311556
  132.4 7.3 %copy-start.2 = (bf16[1,6144,256]{2,1,0:T(8,128)(2,1)S(1)}, bf16[1,6144,256]{2,1,0:T(8,128)(2,1)}, u32[]{:S(2)}) copy-start(bf16[1,6144,256]{2,1,0:T(8,128)(2,1)} %param.10) | copy-start | bytes 9437188
  143.2 11.1 %collective-permute-start = (bf16[256,768]{0,1:T(8,128)(2,1)}, bf16[256,768]{0,1:T(8,128)(2,1)S(1)}, u32[]{:S(2)}, u32[]{:S(2)}) collective-permute-start(bf16[256,768]{0,1:T(8,128)(2,1)} %fusion.13), channel_id=1, source_target_pairs={{0,1},{1,2},{2,3},{3,0},{4,5},{5,6},{6,7},{7,4},{8,9},{9,10},{10,1... | collective-permute-start | bytes 1179656 | tf_op jit(solution)/shard_map/ppermute | solution.py:65
  143.4 10.9 %collective-permute-start.1 = (bf16[256,768]{0,1:T(8,128)(2,1)}, bf16[256,768]{0,1:T(8,128)(2,1)}, u32[]{:S(2)}, u32[]{:S(2)}) collective-permute-start(bf16[256,768]{0,1:T(8,128)(2,1)} %fusion.13), channel_id=1, source_target_pairs={{0,3},{1,0},{2,1},{3,2},{4,7},{5,4},{6,5},{7,6},{8,11},{9,8},{10,9... | collective-permute-start | bytes 1179656 | tf_op jit(solution)/shard_map/ppermute | solution.py:66
  154.3 8.0 %collective-permute-start.2 = (bf16[256,384]{0,1:T(8,128)(2,1)S(1)}, bf16[256,384]{0,1:T(8,128)(2,1)S(1)}, u32[]{:S(2)}, u32[]{:S(2)}) collective-permute-start(bf16[256,384]{0,1:T(8,128)(2,1)S(1)} %slice.30), channel_id=1, source_target_pairs={{0,1},{1,2},{2,3},{3,0},{4,5},{5,6},{6,7},{7,4},{8,9},{9,10},{10,1... | collective-permute-start | bytes 589832 | tf_op jit(solution)/shard_map/ppermute | solution.py:67
  155.3 6.9 %collective-permute-start.3 = (bf16[256,384]{0,1:T(8,128)(2,1)S(1)}, bf16[256,384]{0,1:T(8,128)(2,1)S(1)}, u32[]{:S(2)}, u32[]{:S(2)}) collective-permute-start(bf16[256,384]{0,1:T(8,128)(2,1)S(1)} %slice.31), channel_id=1, source_target_pairs={{0,3},{1,0},{2,1},{3,2},{4,7},{5,4},{6,5},{7,6},{8,11},{9,8},{10,9... | collective-permute-start | bytes 589832 | tf_op jit(solution)/shard_map/ppermute | solution.py:68
  206.6 16.7 %all-to-all-start.2 = ((bf16[8,192,96]{2,1,0:T(8,128)(2,1)}), bf16[8,192,96]{2,1,0:T(8,128)(2,1)S(1)}, u32[]{:S(2)}, u32[]{:S(2)}) async-start(bf16[8,192,96]{2,1,0:T(8,128)(2,1)} %bitcast.78), calls=%async_computation.3 | async-start | bytes 786432 | tf_op jit(solution)/shard_map/all_to_all | solution.py:77
Sparse Core Ops, SparseCore 0:
  26.5 105.8 all-gather.1
  166.0 38.3 reduce-scatter.1

commit v2 on v1

v2 whole, which is shorter than its diff:
```python
import jax
import jax.numpy as jnp
from jax import lax
from jax.experimental import pallas as pl
from jax.experimental.pallas import tpu as pltpu
from jax.sharding import Mesh
from jax.sharding import PartitionSpec as P


NZ = 8
NX = 4


def ring(n, d):
    return [(i, (i + d) % n) for i in range(n)]


def send(value, axis, d):
    return lax.ppermute(value, axis, ring(NZ if axis == "z" else NX, d))


def slot_onehots(ids, experts, cap):
    rows = ids.shape[0]
    lanes = jnp.arange(experts, dtype=jnp.int32)[None, :]
    first = ids[:, 0:1] == lanes
    second = ids[:, 1:2] == lanes
    named = (first | second).astype(jnp.bfloat16)
    i = jnp.arange(rows, dtype=jnp.int32)
    lower = (i[:, None] > i[None, :]).astype(jnp.bfloat16)
    before = jnp.dot(lower, named, preferred_element_type=jnp.float32).astype(jnp.int32)
    position = jnp.arange(cap, dtype=jnp.int32)[None, None, :]
    hit = before[:, :, None] == position
    return first, second, hit


def relayout_down(w_down):
    _, width, model = w_down.shape
    block = model // NZ
    piece = block // NX

    def body(w_ref, out_ref):
        turned = w_ref[0].T
        for x in range(NX):
            out_ref[x, 0] = turned[x * piece:(x + 1) * piece]

    return pl.pallas_call(
        body,
        grid=(NZ,),
        in_specs=[pl.BlockSpec((1, width, block), lambda k: (0, 0, k))],
        out_specs=pl.BlockSpec((NX, 1, piece, width), lambda k: (0, k, 0, 0)),
        out_shape=jax.ShapeDtypeStruct((NX, NZ, piece, width), w_down.dtype),
        name="relayout_down",
    )(w_down)


def down_parts(downs, hidden):
    _, _, piece, width = downs.shape
    slots = hidden.shape[1]

    def body(down_ref, hidden_ref, out_ref, turned_ref):
        @pl.when(pl.program_id(0) == 0)
        def _():
            for x in range(NX):
                turned_ref[x] = hidden_ref[x].T

        total = jnp.zeros((piece, slots), jnp.float32)
        for x in range(NX):
            total += jnp.dot(down_ref[x, 0], turned_ref[x], preferred_element_type=jnp.float32)
        out_ref[...] = total.astype(jnp.bfloat16)

    return pl.pallas_call(
        body,
        grid=(NZ,),
        in_specs=[
            pl.BlockSpec((NX, 1, piece, width), lambda k: (0, k, 0, 0)),
            pl.BlockSpec((NX, slots, width), lambda k: (0, 0, 0)),
        ],
        out_specs=pl.BlockSpec((piece, slots), lambda k: (k, 0)),
        out_shape=jax.ShapeDtypeStruct((NZ * piece, slots), jnp.bfloat16),
        scratch_shapes=[pltpu.VMEM((NX, width, slots), jnp.bfloat16)],
        name="down_parts",
    )(downs, hidden)


def times(block, weight):
    return lax.dot_general(
        block, weight, (((0,), (0,)), ((), ())), preferred_element_type=jnp.float32
    )


def gather_x(value):
    return lax.all_to_all(
        jnp.broadcast_to(value[None], (NX,) + value.shape), "x", 0, 0, tiled=True
    )


def layer(tokens, expert_ids, gate_prob, w_gate, w_up, w_down):
    experts = 8
    rows, columns = tokens.shape
    cap = 3 * rows // experts
    slots = experts * cap
    width = w_gate.shape[2]
    z = lax.axis_index("z")

    first, second, hit = slot_onehots(expert_ids, experts, cap)
    pick = (hit & (first | second)[:, :, None]).astype(jnp.bfloat16).reshape(rows, slots)
    weight = (
        jnp.where(first, gate_prob[:, 0:1], 0.0) + jnp.where(second, gate_prob[:, 1:2], 0.0)
    )
    mix = jnp.where(hit, weight[:, :, None], 0.0).reshape(rows, slots)

    sending = jnp.dot(tokens.T, pick, preferred_element_type=jnp.float32).astype(jnp.bfloat16)
    sending = sending.reshape(columns, experts, cap).transpose(1, 0, 2)
    arrived = lax.all_to_all(sending, ("y", "c"), split_axis=0, concat_axis=0, tiled=True)
    arrived = arrived.transpose(1, 0, 2).reshape(columns, slots)
    cut = slots // 3
    piece_b = lax.all_gather(arrived[:, cut:], ("z", "x"), axis=0, tiled=True)

    a0 = gather_x(arrived[:, :cut]).reshape(NX * columns, cut)
    blocks = {0: a0}
    right, left = a0, a0
    for k in range(1, 4):
        right = send(right, "z", 1)
        left = send(left, "z", -1)
        blocks[-k] = right
        blocks[k] = left
    mid = NX * columns // 2
    far = (send(right[:mid], "z", 1), send(left[mid:], "z", -1))

    down = relayout_down(w_down)
    downs = lax.all_to_all(down, "x", split_axis=0, concat_axis=0, tiled=True)

    def gated_a(w):
        w = w[0].reshape(NZ, NX * columns, width)
        total = None
        for k in (0, 1, -1, 2, -2, 3, -3, 4):
            index = ((z + k) & (NZ - 1), 0, 0)
            wk = lax.dynamic_slice(w, index, (1,) + w.shape[1:], allow_negative_indices=False)[0]
            if k == 4:
                term = times(far[0], wk[:mid]) + times(far[1], wk[mid:])
            else:
                term = times(blocks[k], wk)
            total = term if total is None else total + term
        return total

    hidden_a = (jax.nn.silu(gated_a(w_gate)) * gated_a(w_up)).astype(jnp.bfloat16)
    all_a = gather_x(hidden_a)
    part_a = down_parts(downs, all_a)
    sum_a = lax.psum_scatter(part_a, "z", scatter_dimension=0, tiled=True)
    gate_b = times(piece_b, w_gate[0])
    up_b = times(piece_b, w_up[0])
    hidden_b = (jax.nn.silu(gate_b) * up_b).astype(jnp.bfloat16)
    all_b = gather_x(hidden_b)
    part_b = down_parts(downs, all_b)
    sum_b = lax.psum_scatter(part_b, "z", scatter_dimension=0, tiled=True)

    back = jnp.concatenate([sum_a, sum_b], axis=1)
    back = back.reshape(columns, experts, cap).transpose(1, 0, 2)
    back = lax.all_to_all(back, ("y", "c"), split_axis=0, concat_axis=0, tiled=True)
    table = back.transpose(1, 0, 2).reshape(columns, slots)
    high = lax.reduce_precision(mix, 8, 7)
    low = (mix - high).astype(jnp.bfloat16)
    high = high.astype(jnp.bfloat16)
    last = (((1,), (1,)), ((), ()))
    mixed = lax.dot_general(table, high, last, preferred_element_type=jnp.float32)
    mixed += lax.dot_general(table, low, last, preferred_element_type=jnp.float32)
    return mixed.astype(jnp.bfloat16).T


def solution(mesh):
    grid = Mesh(mesh.devices.reshape(4, 2, NZ, NX), ("y", "c", "z", "x"))
    group = ("y", "c")
    tensor = ("z", "x")
    return jax.shard_map(
        layer,
        mesh=grid,
        in_specs=(
            P(group, tensor),
            P(group, None),
            P(group, None),
            P(group, None, tensor),
            P(group, None, tensor),
            P(group, tensor, None),
        ),
        out_specs=P(group, tensor),
        check_vma=False,
    )
```

time: 234 us -> 265 us (1.13)
  blocking collectives: 13.8 us -> 63.6 us
  waiting for transfers between devices: 144 us -> 98.5 us
  Pallas kernels: 0 us -> 21.3 us
  starting transfers between devices: 19.3 us -> 32.3 us
  local copies, waits for them, and re-layouts: 18.1 us -> 11.7 us
  matrix products: 23.1 us -> 18.7 us
    all_gather x1, waiting for transfers between devices: 92.8 us -> 0.02 us  [layer(): piece_b = lax.all_gather(arrived[:, cut:], ('z', 'x'), axis=0, tiled=True)]
    all_to_all x1 -> x3, blocking collectives: 13.8 us -> 63.6 us  [the longest x1 36.9 us: layer(): downs = lax.all_to_all(down, 'x', split_axis=0, concat_axis=0, tiled=True)]
    pallas_call x0 -> x3, Pallas kernels: none -> 21.3 us  [the longest x2 14.6 us: down_parts(): pl.pallas_call(body, grid=(NZ,), in_specs=[pl.BlockSpec((NX, 1, piece, wi...]
    ppermute x4 -> x8, waiting for transfers between devices: 6.37 us -> 26.7 us  [send(): return lax.ppermute(value, axis, ring(NZ if axis == 'z' else NX, d))]
    all_to_all x2 -> x3, waiting for transfers between devices: 6.34 us -> 20.2 us  [the longest x2 13.9 us: gather_x(): lax.all_to_all(jnp.broadcast_to(value[None], (NX,) + value.shape), 'x', 0...]
    reduce_scatter x1 -> x2, waiting for transfers between devices: 38.5 us -> 51.5 us  [the longest x1 42.1 us: layer(): sum_b = lax.psum_scatter(part_b, 'z', scatter_dimension=0, tiled=True)]
    ppermute x4 -> x8, starting transfers between devices: 5.67 us -> 14.4 us  [send(): return lax.ppermute(value, axis, ring(NZ if axis == 'z' else NX, d))]
    unnamed x7 -> x8, local copies, waits for them, and re-layouts: 6.64 us -> 0.75 us
  transfers between devices with their start and end apart: 8 -> 14, of which waited for: 4 -> 9; matrix products, arithmetic and copies ran while one was open for 11% -> 7% of each run, Pallas kernels for 0% -> 8%
where the time goes in v2:
time: 265 us; the launch traced here: 264 us
  waiting for transfers between devices  98.5 us (37%)
  blocking collectives  63.6 us (24%)
  starting transfers between devices  32.3 us (12%)
  Pallas kernels  21.3 us (8%)
  matrix products  18.7 us (7%)
  between operations  15.1 us (6%)
  local copies, waits for them, and re-layouts  11.7 us (4%)
    reduce_scatter x1, waiting for transfers between devices, layer(): sum_b = lax.psum_scatter(part_b, 'z', scatter_dimension=0, tiled=True)  42.1 us
    all_to_all x1, blocking collectives, layer(): downs = lax.all_to_all(down, 'x', split_axis=0, concat_axis=0, tiled=True)  36.9 us
    ppermute x8, waiting for transfers between devices, send(): return lax.ppermute(value, axis, ring(NZ if axis == 'z' else NX, d))  26.7 us
    pallas_call x2, Pallas kernels, down_parts(): pl.pallas_call(body, grid=(NZ,), in_specs=[pl.BlockSpec((NX, 1, piece, wi...  14.6 us
    ppermute x8, starting transfers between devices, send(): return lax.ppermute(value, axis, ring(NZ if axis == 'z' else NX, d))  14.4 us
    dot_general x20, matrix products, times(): lax.dot_general(block, weight, (((0,), (0,)), ((), ())), preferred_elemen...  14 us
    all_to_all x2, waiting for transfers between devices, gather_x(): lax.all_to_all(jnp.broadcast_to(value[None], (NX,) + value.shape), 'x', 0...  13.9 us
    all_to_all x1, blocking collectives, layer(): lax.all_to_all(sending, ('y', 'c'), split_axis=0, concat_axis=0, tiled=True)  13.8 us
  transfers between devices with their start and end apart: 14, of which 9 were waited for; matrix products, arithmetic and copies ran while one was open for 7% of the time, Pallas kernels for 8%

profile of v2, /device:TPU:1, one launch (start us, length us, event | category | flops | bytes accessed | tf_op | source)
XLA Modules:
  0.0 263.8 jit_solution(15513652690873712113)
XLA Ops:
  8.7 1.9 fusion.10
  10.6 1.4 reshape.161
  12.1 13.8 %all_to_all.30 = bf16[8,192,96]{2,1,0:T(8,128)(2,1)S(1)} all-to-all(bf16[8,192,96]{2,1,0:T(8,128)(2,1)S(1)} %bitcast.145), channel_id=1, replica_groups=mesh['y'=4,'c'=2,'z'=8,'x'=4] {'y','c'}, dimensions={0} | all-to-all | bytes 589824 | tf_op jit(solution)/shard_map/all_to_all | solution.py:114
  27.2 1.6 slice.73
  30.5 4.0 %all-to-all-start.2 = ((bf16[4,192,256]{2,1,0:T(8,128)(2,1)}), bf16[4,192,256]{2,1,0:T(8,128)(2,1)S(1)}, u32[]{:S(2)}, u32[]{:S(2)}) async-start(bf16[4,192,256]{2,1,0:T(8,128)(2,1)} %broadcast_in_dim.60), calls=%async_computation.2 | async-start | bytes 786432 | tf_op jit(solution)/shard_map/all_to_all | solution.py:92
  34.6 6.7 %all-to-all-done.2 = bf16[4,192,256]{2,1,0:T(8,128)(2,1)S(1)} async-done(((bf16[4,192,256]{2,1,0:T(8,128)(2,1)}), bf16[4,192,256]{2,1,0:T(8,128)(2,1)S(1)}, u32[]{:S(2)}, u32[]{:S(2)}) %all-to-all-start.2) | async-done | bytes 393248 | tf_op jit(solution)/shard_map/all_to_all | solution.py:92
  41.3 1.6 collective-permute-start.1
  42.9 3.9 %collective-permute-start = (bf16[768,256]{1,0:T(8,128)(2,1)S(1)}, bf16[768,256]{1,0:T(8,128)(2,1)S(1)}, u32[]{:S(2)}, u32[]{:S(2)}) collective-permute-start(bf16[768,256]{1,0:T(8,128)(2,1)S(1)} %bitcast.133), channel_id=1, source_target_pairs={{0,28},{4,0},{8,4},{12,8},{16,12},{20,16},{24,20},{28,24},{1,29},{... | collective-permute-start | bytes 1179656 | tf_op jit(solution)/shard_map/ppermute | solution.py:19
  46.9 1.3 fusion.32
  48.5 8.2 %collective-permute-done.1 = bf16[768,256]{1,0:T(8,128)(2,1)S(1)} collective-permute-done((bf16[768,256]{1,0:T(8,128)(2,1)S(1)}, bf16[768,256]{1,0:T(8,128)(2,1)S(1)}, u32[]{:S(2)}, u32[]{:S(2)}) %collective-permute-start.1) | collective-permute-done | bytes 393248 | tf_op jit(solution)/shard_map/ppermute | solution.py:19
  56.8 3.1 %collective-permute-start.2 = (bf16[768,256]{1,0:T(8,128)(2,1)S(1)}, bf16[768,256]{1,0:T(8,128)(2,1)S(1)}, u32[]{:S(2)}, u32[]{:S(2)}) collective-permute-start(bf16[768,256]{1,0:T(8,128)(2,1)S(1)} %collective-permute-done), channel_id=1, source_target_pairs={{0,28},{4,0},{8,4},{12,8},{16,12},{20,16},{24,20},{28,24},{1,29},{... | collective-permute-start | bytes 1179656 | tf_op jit(solution)/shard_map/ppermute | solution.py:19
  62.2 7.3 %collective-permute-done.3 = bf16[768,256]{1,0:T(8,128)(2,1)S(1)} collective-permute-done((bf16[768,256]{1,0:T(8,128)(2,1)S(1)}, bf16[768,256]{1,0:T(8,128)(2,1)S(1)}, u32[]{:S(2)}, u32[]{:S(2)}) %collective-permute-start.3) | collective-permute-done | bytes 393248 | tf_op jit(solution)/shard_map/ppermute | solution.py:19
  69.5 2.7 %collective-permute-start.4 = (bf16[768,256]{1,0:T(8,128)(2,1)S(1)}, bf16[768,256]{1,0:T(8,128)(2,1)S(1)}, u32[]{:S(2)}, u32[]{:S(2)}) collective-permute-start(bf16[768,256]{1,0:T(8,128)(2,1)S(1)} %collective-permute-done.2), channel_id=1, source_target_pairs={{0,28},{4,0},{8,4},{12,8},{16,12},{20,16},{24,20},{28,24},{1,29},{... | collective-permute-start | bytes 1179656 | tf_op jit(solution)/shard_map/ppermute | solution.py:19
  73.4 4.9 %collective-permute-done.5 = bf16[768,256]{1,0:T(8,128)(2,1)S(1)} collective-permute-done((bf16[768,256]{1,0:T(8,128)(2,1)S(1)}, bf16[768,256]{1,0:T(8,128)(2,1)S(1)}, u32[]{:S(2)}, u32[]{:S(2)}) %collective-permute-start.5) | collective-permute-done | bytes 393248 | tf_op jit(solution)/shard_map/ppermute | solution.py:19
  78.4 2.9 %collective-permute-start.7 = (bf16[384,256]{1,0:T(8,128)(2,1)S(1)}, bf16[384,256]{1,0:T(8,128)(2,1)S(1)}, u32[]{:S(2)}, u32[]{:S(2)}) collective-permute-start(bf16[384,256]{1,0:T(8,128)(2,1)S(1)} %slice.72), channel_id=1, source_target_pairs={{0,28},{4,0},{8,4},{12,8},{16,12},{20,16},{24,20},{28,24},{1,29},{... | collective-permute-start | bytes 589832 | tf_op jit(solution)/shard_map/ppermute | solution.py:19
  82.0 6.2 %collective-permute-done.7 = bf16[384,256]{1,0:T(8,128)(2,1)S(1)} collective-permute-done((bf16[384,256]{1,0:T(8,128)(2,1)S(1)}, bf16[384,256]{1,0:T(8,128)(2,1)S(1)}, u32[]{:S(2)}, u32[]{:S(2)}) %collective-permute-start.7) | collective-permute-done | bytes 196640 | tf_op jit(solution)/shard_map/ppermute | solution.py:19
  90.8 4.9 %all-to-all-start.3 = ((bf16[4,256,256]{2,1,0:T(8,128)(2,1)}), bf16[4,256,256]{2,1,0:T(8,128)(2,1)}, u32[]{:S(2)}, u32[]{:S(2)}) async-start(bf16[4,256,256]{2,1,0:T(8,128)(2,1)} %broadcast_in_dim.61), calls=%async_computation.3 | async-start | bytes 1048576 | tf_op jit(solution)/shard_map/all_to_all | solution.py:92
  95.7 6.7 %relayout_down.1 = bf16[4,8,192,256]{3,2,1,0:T(8,128)(2,1)} custom-call(bf16[1,256,6144]{2,1,0:T(8,128)(2,1)} %w_ref.1), custom_call_target="tpu_custom_call" | custom-call | tf_op jit(solution)/shard_map/relayout_down/pallas_call | solution.py:46
  102.3 7.2 %all-to-all-done.3.hidden_ref = bf16[4,256,256]{2,1,0:T(8,128)(2,1)} async-done(((bf16[4,256,256]{2,1,0:T(8,128)(2,1)}), bf16[4,256,256]{2,1,0:T(8,128)(2,1)}, u32[]{:S(2)}, u32[]{:S(2)}) %all-to-all-start.3) | async-done | bytes 524320 | tf_op jit(solution)/shard_map/all_to_all | solution.py:92
  109.5 36.9 %all_to_all.31.down_ref = bf16[4,8,192,256]{3,2,1,0:T(8,128)(2,1)} all-to-all(bf16[4,8,192,256]{3,2,1,0:T(8,128)(2,1)} %relayout_down.1), channel_id=1, replica_groups=mesh['y'=4,'c'=2,'z'=8,'x'=4] {'x'}, dimensions={0} | all-to-all | bytes 6291456 | tf_op jit(solution)/shard_map/all_to_all | solution.py:131
  146.4 6.9 %down_parts.2 = bf16[1536,256]{1,0:T(8,128)(2,1)} custom-call(bf16[4,8,192,256]{3,2,1,0:T(8,128)(2,1)} %all_to_all.31.down_ref, bf16[4,256,256]{2,1,0:T(8,128)(2,1)} %all-to-all-done.3.hidden_ref), custom_call_target="tpu_custom_call" | custom-call | tf_op jit(solution)/shard_map/down_parts/pallas_call | solution.py:71
  153.5 4.8 %fusion.2 = f32[512,256]{1,0:T(8,128)S(1)} fusion(bf16[6144,512]{1,0:T(8,128)(2,1)} %all-gather.2.cloned.1.call-done, bf16[1,6144,256]{2,1,0:T(8,128)(2,1)S(1)} %copy-done), kind=kOutput, calls=%fused_computation.2 | convolution fusion | flops 1610612736 | bytes 9961472 | tf_op jit(solution)/shard_map/dot_general | solution.py:86
  159.0 1.8 fusion.7
  160.9 12.9 %all_to_all.32.hidden_ref = bf16[4,512,256]{2,1,0:T(8,128)(2,1)} all-to-all(bf16[4,512,256]{2,1,0:T(8,128)(2,1)S(1)} %broadcast_in_dim.62), channel_id=1, replica_groups=mesh['y'=4,'c'=2,'z'=8,'x'=4] {'x'}, dimensions={0} | all-to-all | bytes 2097152 | tf_op jit(solution)/shard_map/all_to_all | solution.py:92
  173.8 7.8 %down_parts.3 = bf16[1536,512]{1,0:T(8,128)(2,1)} custom-call(bf16[4,8,192,256]{3,2,1,0:T(8,128)(2,1)} %all_to_all.31.down_ref, bf16[4,512,256]{2,1,0:T(8,128)(2,1)} %all_to_all.32.hidden_ref), custom_call_target="tpu_custom_call" | custom-call | tf_op jit(solution)/shard_map/down_parts/pallas_call | solution.py:71
  181.5 9.4 %reduce-scatter.3.cloned.1.call-done = bf16[192,256]{1,0:T(8,128)(2,1)} async-done(((bf16[1536,256]{1,0:T(8,128)(2,1)}), bf16[192,256]{1,0:T(8,128)(2,1)}) %reduce-scatter.3.cloned.1.call-update) | async-done | bytes 98320 | tf_op jit(solution)/shard_map/reduce_scatter | solution.py:149
  190.9 42.1 %reduce-scatter.5.cloned.1.call-done = bf16[192,512]{1,0:T(8,128)(2,1)} async-done(((bf16[1536,512]{1,0:T(8,128)(2,1)}), bf16[192,512]{1,0:T(8,128)(2,1)}) %reduce-scatter.5.cloned.1.call-update) | async-done | bytes 196624 | tf_op jit(solution)/shard_map/reduce_scatter | solution.py:155
  233.1 1.7 pad_maximum_fusion
  234.8 1.4 reshape.164
  237.0 8.9 %all-to-all-start.5 = ((bf16[8,192,96]{2,1,0:T(8,128)(2,1)}), bf16[8,192,96]{2,1,0:T(8,128)(2,1)S(1)}, u32[]{:S(2)}, u32[]{:S(2)}) async-start(bf16[8,192,96]{2,1,0:T(8,128)(2,1)} %bitcast.121), calls=%async_computation.7 | async-start | bytes 786432 | tf_op jit(solution)/shard_map/all_to_all | solution.py:159
  247.3 6.3 %all-to-all-done.5 = bf16[8,192,96]{2,1,0:T(8,128)(2,1)S(1)} async-done(((bf16[8,192,96]{2,1,0:T(8,128)(2,1)}), bf16[8,192,96]{2,1,0:T(8,128)(2,1)S(1)}, u32[]{:S(2)}, u32[]{:S(2)}) %all-to-all-start.5) | async-done | bytes 294944 | tf_op jit(solution)/shard_map/all_to_all | solution.py:159
  254.7 1.6 fusion.18
  (58 shorter events, 15.6 us)
Async XLA Ops:
  7.4 40.8 %copy-start = (bf16[1,6144,256]{2,1,0:T(8,128)(2,1)S(1)}, bf16[1,6144,256]{2,1,0:T(8,128)(2,1)}, u32[]{:S(2)}) copy-start(bf16[1,6144,256]{2,1,0:T(8,128)(2,1)} %param.9) | copy-start | bytes 9437188
  7.4 146.1 %all-gather.2.cloned.1.call-start = ((), (), s32[]{:S(2)}) async-start(), calls=%async_computation.9 | async-start | bytes 6488064 | tf_op jit(solution)/shard_map/all_gather | solution.py:117
  30.5 10.7 %all-to-all-start.2 = ((bf16[4,192,256]{2,1,0:T(8,128)(2,1)}), bf16[4,192,256]{2,1,0:T(8,128)(2,1)S(1)}, u32[]{:S(2)}, u32[]{:S(2)}) async-start(bf16[4,192,256]{2,1,0:T(8,128)(2,1)} %broadcast_in_dim.60), calls=%async_computation.2 | async-start | bytes 786432 | tf_op jit(solution)/shard_map/all_to_all | solution.py:92
  41.3 20.6 %copy-start.2 = (bf16[1,6144,256]{2,1,0:T(8,128)(2,1)S(1)}, bf16[1,6144,256]{2,1,0:T(8,128)(2,1)}, u32[]{:S(2)}) copy-start(bf16[1,6144,256]{2,1,0:T(8,128)(2,1)} %param.10) | copy-start | bytes 9437188
  41.3 15.5 %collective-permute-start.1 = (bf16[768,256]{1,0:T(8,128)(2,1)S(1)}, bf16[768,256]{1,0:T(8,128)(2,1)S(1)}, u32[]{:S(2)}, u32[]{:S(2)}) collective-permute-start(bf16[768,256]{1,0:T(8,128)(2,1)S(1)} %bitcast.132), channel_id=1, source_target_pairs={{0,4},{4,8},{8,12},{12,16},{16,20},{20,24},{24,28},{28,0},{1,5},{5... | collective-permute-start | bytes 1179656 | tf_op jit(solution)/shard_map/ppermute | solution.py:19
  42.9 13.8 %collective-permute-start = (bf16[768,256]{1,0:T(8,128)(2,1)S(1)}, bf16[768,256]{1,0:T(8,128)(2,1)S(1)}, u32[]{:S(2)}, u32[]{:S(2)}) collective-permute-start(bf16[768,256]{1,0:T(8,128)(2,1)S(1)} %bitcast.133), channel_id=1, source_target_pairs={{0,28},{4,0},{8,4},{12,8},{16,12},{20,16},{24,20},{28,24},{1,29},{... | collective-permute-start | bytes 1179656 | tf_op jit(solution)/shard_map/ppermute | solution.py:19
  56.7 12.7 %collective-permute-start.3 = (bf16[768,256]{1,0:T(8,128)(2,1)S(1)}, bf16[768,256]{1,0:T(8,128)(2,1)S(1)}, u32[]{:S(2)}, u32[]{:S(2)}) collective-permute-start(bf16[768,256]{1,0:T(8,128)(2,1)S(1)} %collective-permute-done.1), channel_id=1, source_target_pairs={{0,4},{4,8},{8,12},{12,16},{16,20},{20,24},{24,28},{28,0},{1,5},{5... | collective-permute-start | bytes 1179656 | tf_op jit(solution)/shard_map/ppermute | solution.py:19
  56.8 12.7 %collective-permute-start.2 = (bf16[768,256]{1,0:T(8,128)(2,1)S(1)}, bf16[768,256]{1,0:T(8,128)(2,1)S(1)}, u32[]{:S(2)}, u32[]{:S(2)}) collective-permute-start(bf16[768,256]{1,0:T(8,128)(2,1)S(1)} %collective-permute-done), channel_id=1, source_target_pairs={{0,28},{4,0},{8,4},{12,8},{16,12},{20,16},{24,20},{28,24},{1,29},{... | collective-permute-start | bytes 1179656 | tf_op jit(solution)/shard_map/ppermute | solution.py:19
  69.5 8.8 %collective-permute-start.5 = (bf16[768,256]{1,0:T(8,128)(2,1)S(1)}, bf16[768,256]{1,0:T(8,128)(2,1)S(1)}, u32[]{:S(2)}, u32[]{:S(2)}) collective-permute-start(bf16[768,256]{1,0:T(8,128)(2,1)S(1)} %collective-permute-done.3), channel_id=1, source_target_pairs={{0,4},{4,8},{8,12},{12,16},{16,20},{20,24},{24,28},{28,0},{1,5},{5... | collective-permute-start | bytes 1179656 | tf_op jit(solution)/shard_map/ppermute | solution.py:19
  69.5 8.9 %collective-permute-start.4 = (bf16[768,256]{1,0:T(8,128)(2,1)S(1)}, bf16[768,256]{1,0:T(8,128)(2,1)S(1)}, u32[]{:S(2)}, u32[]{:S(2)}) collective-permute-start(bf16[768,256]{1,0:T(8,128)(2,1)S(1)} %collective-permute-done.2), channel_id=1, source_target_pairs={{0,28},{4,0},{8,4},{12,8},{16,12},{20,16},{24,20},{28,24},{1,29},{... | collective-permute-start | bytes 1179656 | tf_op jit(solution)/shard_map/ppermute | solution.py:19
  78.3 10.4 %collective-permute-start.6 = (bf16[384,256]{1,0:T(8,128)(2,1)S(1)}, bf16[384,256]{1,0:T(8,128)(2,1)S(1)}, u32[]{:S(2)}, u32[]{:S(2)}) collective-permute-start(bf16[384,256]{1,0:T(8,128)(2,1)S(1)} %slice.71), channel_id=1, source_target_pairs={{0,4},{4,8},{8,12},{12,16},{16,20},{20,24},{24,28},{28,0},{1,5},{5... | collective-permute-start | bytes 589832 | tf_op jit(solution)/shard_map/ppermute | solution.py:19
  78.4 9.8 %collective-permute-start.7 = (bf16[384,256]{1,0:T(8,128)(2,1)S(1)}, bf16[384,256]{1,0:T(8,128)(2,1)S(1)}, u32[]{:S(2)}, u32[]{:S(2)}) collective-permute-start(bf16[384,256]{1,0:T(8,128)(2,1)S(1)} %slice.72), channel_id=1, source_target_pairs={{0,28},{4,0},{8,4},{12,8},{16,12},{20,16},{24,20},{28,24},{1,29},{... | collective-permute-start | bytes 589832 | tf_op jit(solution)/shard_map/ppermute | solution.py:19
  90.8 18.7 %all-to-all-start.3 = ((bf16[4,256,256]{2,1,0:T(8,128)(2,1)}), bf16[4,256,256]{2,1,0:T(8,128)(2,1)}, u32[]{:S(2)}, u32[]{:S(2)}) async-start(bf16[4,256,256]{2,1,0:T(8,128)(2,1)} %broadcast_in_dim.61), calls=%async_computation.3 | async-start | bytes 1048576 | tf_op jit(solution)/shard_map/all_to_all | solution.py:92
  95.7 95.2 %reduce-scatter.3.cloned.1.call-start = ((), (), s32[]{:S(2)}) async-start(), calls=%async_computation.8 | async-start | bytes 884736 | tf_op jit(solution)/shard_map/reduce_scatter | solution.py:149
  153.3 79.7 %reduce-scatter.5.cloned.1.call-start = ((), (), s32[]{:S(2)}) async-start(), calls=%async_computation.10 | async-start | bytes 1769472 | tf_op jit(solution)/shard_map/reduce_scatter | solution.py:155
  153.4 4.8 %copy-start.1 = (bf16[6144,512]{1,0:T(8,128)(2,1)S(1)}, bf16[6144,512]{1,0:T(8,128)(2,1)}, u32[]{:S(2)}) copy-start(bf16[6144,512]{1,0:T(8,128)(2,1)} %all-gather.2.cloned.1.call-done) | copy-start | bytes 18874372
  153.4 5.5 %copy-start.3 = (bf16[1,6144,256]{2,1,0:T(8,128)(2,1)S(1)}, bf16[1,6144,256]{2,1,0:T(8,128)(2,1)}, u32[]{:S(2)}) copy-start(bf16[1,6144,256]{2,1,0:T(8,128)(2,1)} %param.10) | copy-start | bytes 9437188
  237.0 16.6 %all-to-all-start.5 = ((bf16[8,192,96]{2,1,0:T(8,128)(2,1)}), bf16[8,192,96]{2,1,0:T(8,128)(2,1)S(1)}, u32[]{:S(2)}, u32[]{:S(2)}) async-start(bf16[8,192,96]{2,1,0:T(8,128)(2,1)} %bitcast.121), calls=%async_computation.7 | async-start | bytes 786432 | tf_op jit(solution)/shard_map/all_to_all | solution.py:159
Sparse Core Ops, SparseCore 0:
  29.0 94.2 all-gather.1
Sparse Core Ops, SparseCore 1:
  153.4 37.4 reduce-scatter.2
  193.4 39.7 reduce-scatter.4

commit v3 on v2

--- a/solution.py
+++ b/solution.py
@@ -33,29 +33,33 @@
     return first, second, hit
 
 
-def relayout_down(w_down):
+def relayout_down(place, w_down):
     _, width, model = w_down.shape
     block = model // NZ
     piece = block // NX
 
-    def body(w_ref, out_ref):
+    def body(place_ref, w_ref, out_ref):
         turned = w_ref[0].T
         for x in range(NX):
             out_ref[x, 0] = turned[x * piece:(x + 1) * piece]
 
     return pl.pallas_call(
         body,
-        grid=(NZ,),
-        in_specs=[pl.BlockSpec((1, width, block), lambda k: (0, 0, k))],
-        out_specs=pl.BlockSpec((NX, 1, piece, width), lambda k: (0, k, 0, 0)),
+        grid_spec=pltpu.PrefetchScalarGridSpec(
+            num_scalar_prefetch=1,
+            grid=(NZ,),
+            in_specs=[pl.BlockSpec((1, width, block), lambda k, s: (0, 0, (s[0] + k) & (NZ - 1)))],
+            out_specs=pl.BlockSpec((NX, 1, piece, width), lambda k, s: (0, k, 0, 0)),
+        ),
         out_shape=jax.ShapeDtypeStruct((NX, NZ, piece, width), w_down.dtype),
         name="relayout_down",
-    )(w_down)
-
-
-def down_parts(downs, hidden):
+    )(place, w_down)
+
+
+def down_parts(downs, hidden, order):
     _, _, piece, width = downs.shape
     slots = hidden.shape[1]
+    first = order[0]
 
     def body(down_ref, hidden_ref, out_ref, turned_ref):
         @pl.when(pl.program_id(0) == 0)
@@ -66,31 +70,52 @@
         total = jnp.zeros((piece, slots), jnp.float32)
         for x in range(NX):
             total += jnp.dot(down_ref[x, 0], turned_ref[x], preferred_element_type=jnp.float32)
-        out_ref[...] = total.astype(jnp.bfloat16)
+        out_ref[0] = total.astype(jnp.bfloat16)
 
     return pl.pallas_call(
         body,
-        grid=(NZ,),
+        grid=(len(order),),
         in_specs=[
-            pl.BlockSpec((NX, 1, piece, width), lambda k: (0, k, 0, 0)),
+            pl.BlockSpec((NX, 1, piece, width), lambda k: (0, (k + first) & (NZ - 1), 0, 0)),
             pl.BlockSpec((NX, slots, width), lambda k: (0, 0, 0)),
         ],
-        out_specs=pl.BlockSpec((piece, slots), lambda k: (k, 0)),
-        out_shape=jax.ShapeDtypeStruct((NZ * piece, slots), jnp.bfloat16),
+        out_specs=pl.BlockSpec((1, piece, slots), lambda k: (k, 0, 0)),
+        out_shape=jax.ShapeDtypeStruct((len(order), piece, slots), jnp.bfloat16),
         scratch_shapes=[pltpu.VMEM((NX, width, slots), jnp.bfloat16)],
         name="down_parts",
     )(downs, hidden)
 
 
+def scatter_z(parts):
+    half = parts[4].shape[0] // 2
+
+    def add(a, b):
+        return (a.astype(jnp.float32) + b.astype(jnp.float32)).astype(jnp.bfloat16)
+
+    right = send(parts[4][:half], "z", 1)
+    left = send(parts[4][half:], "z", -1)
+    right = jnp.concatenate([add(parts[3][:half], right), parts[3][half:]], axis=0)
+    left = jnp.concatenate([parts[5][:half], add(parts[5][half:], left)], axis=0)
+    right = send(right, "z", 1)
+    left = send(left, "z", -1)
+    right = send(add(parts[2], right), "z", 1)
+    left = send(add(parts[6], left), "z", -1)
+    right = send(add(parts[1], right), "z", 1)
+    left = send(add(parts[7], left), "z", -1)
+    total = parts[0].astype(jnp.float32) + right.astype(jnp.float32) + left.astype(jnp.float32)
+    return total.astype(jnp.bfloat16)
+
+
 def times(block, weight):
     return lax.dot_general(
         block, weight, (((0,), (0,)), ((), ())), preferred_element_type=jnp.float32
     )
 
 
-def gather_x(value):
+def gather(value, axis):
+    n = NZ if axis == "z" else NX
     return lax.all_to_all(
-        jnp.broadcast_to(value[None], (NX,) + value.shape), "x", 0, 0, tiled=True
+        jnp.broadcast_to(value[None], (n,) + value.shape), axis, 0, 0, tiled=True
     )
 
 
@@ -101,6 +126,7 @@
     slots = experts * cap
     width = w_gate.shape[2]
     z = lax.axis_index("z")
+    x = lax.axis_index("x")
 
     first, second, hit = slot_onehots(expert_ids, experts, cap)
     pick = (hit & (first | second)[:, :, None]).astype(jnp.bfloat16).reshape(rows, slots)
@@ -113,10 +139,8 @@
     sending = sending.reshape(columns, experts, cap).transpose(1, 0, 2)
     arrived = lax.all_to_all(sending, ("y", "c"), split_axis=0, concat_axis=0, tiled=True)
     arrived = arrived.transpose(1, 0, 2).reshape(columns, slots)
-    cut = slots // 3
-    piece_b = lax.all_gather(arrived[:, cut:], ("z", "x"), axis=0, tiled=True)
-
-    a0 = gather_x(arrived[:, :cut]).reshape(NX * columns, cut)
+    cut = 2 * slots // 3
+    a0 = gather(arrived[:, :cut], "x").reshape(NX * columns, cut)
     blocks = {0: a0}
     right, left = a0, a0
     for k in range(1, 4):
@@ -127,7 +151,13 @@
     mid = NX * columns // 2
     far = (send(right[:mid], "z", 1), send(left[mid:], "z", -1))
 
-    down = relayout_down(w_down)
+    b0 = gather(arrived[:, cut:], "z").reshape(NZ * columns, slots - cut)
+    b_left = send(b0, "x", 1)
+    b_right = send(b0, "x", -1)
+    bmid = NZ * columns // 2
+    b_far = (send(b_left[:bmid], "x", 1), send(b_right[bmid:], "x", -1))
+
+    down = relayout_down(z.astype(jnp.int32)[None], w_down)
     downs = lax.all_to_all(down, "x", split_axis=0, concat_axis=0, tiled=True)
 
     def gated_a(w):
@@ -143,18 +173,31 @@
             total = term if total is None else total + term
         return total
 
+    def gated_b(w):
+        w = w[0].reshape(NZ, NX, columns, width).transpose(1, 0, 2, 3).reshape(NX, NZ * columns, width)
+
+        def at(k):
+            index = ((x + k) & (NX - 1), 0, 0)
+            return lax.dynamic_slice(
+                w, index, (1,) + w.shape[1:], allow_negative_indices=False
+            )[0]
+
+        total = times(b0, at(0)) + times(b_right, at(1)) + times(b_left, at(3))
+        opposite = at(2)
+        return total + (times(b_far[0], opposite[:bmid]) + times(b_far[1], opposite[bmid:]))
+
+    hidden_b = (jax.nn.silu(gated_b(w_gate)) * gated_b(w_up)).astype(jnp.bfloat16)
+    all_b = gather(hidden_b, "x")
+    part_b = down_parts(downs, all_b, (0, 1, 2, 3, 4, 5, 6, 7))
     hidden_a = (jax.nn.silu(gated_a(w_gate)) * gated_a(w_up)).astype(jnp.bfloat16)
-    all_a = gather_x(hidden_a)
-    part_a = down_parts(downs, all_a)
-    sum_a = lax.psum_scatter(part_a, "z", scatter_dimension=0, tiled=True)
-    gate_b = times(piece_b, w_gate[0])
-    up_b = times(piece_b, w_up[0])
-    hidden_b = (jax.nn.silu(gate_b) * up_b).astype(jnp.bfloat16)
-    all_b = gather_x(hidden_b)
-    part_b = down_parts(downs, all_b)
-    sum_b = lax.psum_scatter(part_b, "z", scatter_dimension=0, tiled=True)
-
-    back = jnp.concatenate([sum_a, sum_b], axis=1)
+    all_a = gather(hidden_a, "x")
+    early = down_parts(downs, all_a, (3, 4, 5))
+    late = down_parts(downs, all_a, (6, 7, 0, 1, 2))
+    parts = {}
+    for k in range(NZ):
+        part_a = early[k - 3] if 3 <= k <= 5 else late[(k - 6) % NZ]
+        parts[k] = jnp.concatenate([part_a, part_b[k]], axis=1)
+    back = scatter_z(parts)
     back = back.reshape(columns, experts, cap).transpose(1, 0, 2)
     back = lax.all_to_all(back, ("y", "c"), split_axis=0, concat_axis=0, tiled=True)
     table = back.transpose(1, 0, 2).reshape(columns, slots)

time: 265 us -> 247 us (0.932)
  blocking collectives: 63.6 us -> 13.8 us
  starting transfers between devices: 32.3 us -> 65.8 us
  between operations: 15.1 us -> 0.61 us
  matrix products: 18.7 us -> 30.5 us
  local copies, waits for them, and re-layouts: 11.7 us -> 20.4 us
  waiting for transfers between devices: 98.5 us -> 90.6 us
    reduce_scatter x2 -> x0, waiting for transfers between devices: 51.5 us -> none  [the longest x1 42.1 us: layer(): sum_b = lax.psum_scatter(part_b, 'z', scatter_dimension=0, tiled=True)]
    all_to_all x2 -> x0, blocking collectives: 49.8 us -> none  [the longest x1 36.9 us: layer(): downs = lax.all_to_all(down, 'x', split_axis=0, concat_axis=0, tiled=True)]
    ppermute x8 -> x20, waiting for transfers between devices: 26.7 us -> 65 us  [send(): return lax.ppermute(value, axis, ring(NZ if axis == 'z' else NX, d))]
    all_to_all x2 -> x5, starting transfers between devices: 8.92 us -> 23.8 us  [the longest x4 20.1 us: gather(): lax.all_to_all(jnp.broadcast_to(value[None], (n,) + value.shape), axis, 0...]
    dot_general x20 -> x28, matrix products: 14 us -> 28.7 us  [times(): lax.dot_general(block, weight, (((0,), (0,)), ((), ())), preferred_elemen...]
    ppermute x8 -> x20, starting transfers between devices: 14.4 us -> 27.5 us  [send(): return lax.ppermute(value, axis, ring(NZ if axis == 'z' else NX, d))]
    transpose x0 -> x2, local copies, waits for them, and re-layouts: none -> 5.8 us  [gated_b(): w[0].reshape(NZ, NX, columns, width).transpose(1, 0, 2, 3)]
    all_to_all x1, starting transfers between devices: 8.93 us -> 14.5 us  [layer(): lax.all_to_all(back, ('y', 'c'), split_axis=0, concat_axis=0, tiled=True)]
  transfers between devices with their start and end apart: 14 -> 26, of which waited for: 9 -> 14; matrix products, arithmetic and copies ran while one was open for 7% -> 15% of each run, Pallas kernels for 8% -> 8%
where the time goes in v3:
time: 247 us; the launch traced here: 246 us
  waiting for transfers between devices  90.6 us (37%)
  starting transfers between devices  65.8 us (27%)
  matrix products  30.5 us (12%)
  Pallas kernels  23.5 us (10%)
  local copies, waits for them, and re-layouts  20.4 us (8%)
  blocking collectives  13.8 us (6%)
    ppermute x20, waiting for transfers between devices, send(): return lax.ppermute(value, axis, ring(NZ if axis == 'z' else NX, d))  65 us
    dot_general x28, matrix products, times(): lax.dot_general(block, weight, (((0,), (0,)), ((), ())), preferred_elemen...  28.7 us
    ppermute x20, starting transfers between devices, send(): return lax.ppermute(value, axis, ring(NZ if axis == 'z' else NX, d))  27.5 us
    all_to_all x4, starting transfers between devices, gather(): lax.all_to_all(jnp.broadcast_to(value[None], (n,) + value.shape), axis, 0...  20.1 us
    all_to_all x4, waiting for transfers between devices, gather(): lax.all_to_all(jnp.broadcast_to(value[None], (n,) + value.shape), axis, 0...  17.9 us
    pallas_call x3, Pallas kernels, down_parts(): pl.pallas_call(body, grid=(len(order),), in_specs=[pl.BlockSpec((NX, 1, p...  16.8 us
    all_to_all x1, starting transfers between devices, layer(): lax.all_to_all(back, ('y', 'c'), split_axis=0, concat_axis=0, tiled=True)  14.5 us
    all_to_all x1, blocking collectives, layer(): lax.all_to_all(sending, ('y', 'c'), split_axis=0, concat_axis=0, tiled=True)  13.8 us
  transfers between devices with their start and end apart: 26, of which 14 were waited for; matrix products, arithmetic and copies ran while one was open for 15% of the time, Pallas kernels for 8%

profile of v3, /device:TPU:1, one launch (start us, length us, event | category | flops | bytes accessed | tf_op | source)
XLA Modules:
  0.0 245.8 jit_solution(9803733372540424710)
XLA Ops:
  2.1 13.8 %all_to_all.35 = bf16[8,192,96]{2,1,0:T(8,128)(2,1)S(1)} all-to-all(bf16[8,192,96]{2,1,0:T(8,128)(2,1)S(1)} %bitcast.225), channel_id=1, replica_groups=mesh['y'=4,'c'=2,'z'=8,'x'=4] {'y','c'}, dimensions={0} | all-to-all | bytes 589824 | tf_op jit(solution)/shard_map/all_to_all | solution.py:140
  19.4 4.2 %all-to-all-start.2 = ((bf16[4,192,512]{2,1,0:T(8,128)(2,1)}), bf16[4,192,512]{2,1,0:T(8,128)(2,1)}, u32[]{:S(2)}, u32[]{:S(2)}) async-start(bf16[4,192,512]{2,1,0:T(8,128)(2,1)} %broadcast_in_dim.70), calls=%async_computation.2 | async-start | bytes 1572864 | tf_op jit(solution)/shard_map/all_to_all | solution.py:117
  24.2 10.8 %all-to-all-done.2 = bf16[4,192,512]{2,1,0:T(8,128)(2,1)} async-done(((bf16[4,192,512]{2,1,0:T(8,128)(2,1)}), bf16[4,192,512]{2,1,0:T(8,128)(2,1)}, u32[]{:S(2)}, u32[]{:S(2)}) %all-to-all-start.2) | async-done | bytes 786464 | tf_op jit(solution)/shard_map/all_to_all | solution.py:117
  36.8 8.2 %all-to-all-start.4 = ((bf16[8,192,256]{2,1,0:T(8,128)(2,1)}), bf16[8,192,256]{2,1,0:T(8,128)(2,1)}, u32[]{:S(2)}, u32[]{:S(2)}) async-start(bf16[8,192,256]{2,1,0:T(8,128)(2,1)} %broadcast_in_dim.72), calls=%async_computation.4 | async-start | bytes 1572864 | tf_op jit(solution)/shard_map/all_to_all | solution.py:117
  49.6 3.9 %copy.19 = bf16[4,8,192,256]{3,2,1,0:T(8,128)(2,1)} copy(bf16[4,8,192,256]{3,2,0,1:T(8,128)(2,1)} %bitcast.215) | data formatting | bytes 6291456 | tf_op jit(solution)/shard_map/transpose | solution.py:177
  53.5 6.6 %relayout_down.1 = bf16[4,8,192,256]{3,2,1,0:T(8,128)(2,1)} custom-call(s32[1]{0:T(128)} %bitcast.4.place_ref, bf16[1,256,6144]{2,1,0:T(8,128)(2,1)} %w_ref.1), custom_call_target="tpu_custom_call" | custom-call | tf_op jit(solution)/shard_map/relayout_down/pallas_call | solution.py:46
  62.5 2.5 %fusion.44 = f32[512,256]{1,0:T(8,128)} fusion(bf16[768,512]{1,0:T(8,128)(2,1)} %bitcast.10, bf16[8,768,256]{2,1,0:T(8,128)(2,1)} %bitcast.216, s32[]{:T(128)S(6)} %and.64), kind=kOutput, calls=%fused_computation.76 | convolution fusion | flops 201326592 | bytes 1703940 | tf_op jit(solution)/shard_map/dot_general | solution.py:110
  64.9 2.4 all-to-all-done.4
  67.3 3.7 %all-to-all-start = ((bf16[4,8,192,256]{3,2,1,0:T(8,128)(2,1)}), bf16[4,8,192,256]{3,2,1,0:T(8,128)(2,1)S(1)}, u32[]{:S(2)}, u32[]{:S(2)}) async-start(bf16[4,8,192,256]{3,2,1,0:T(8,128)(2,1)} %relayout_down.1), calls=%async_computation | async-start | bytes 6291456 | tf_op jit(solution)/shard_map/all_to_all | solution.py:161
  71.1 2.6 %collective-permute-start.8 = (bf16[1536,256]{1,0:T(8,128)(2,1)}, bf16[1536,256]{1,0:T(8,128)(2,1)S(1)}, u32[]{:S(2)}, u32[]{:S(2)}) collective-permute-start(bf16[1536,256]{1,0:T(8,128)(2,1)} %bitcast.32), channel_id=1, source_target_pairs={{0,3},{1,0},{2,1},{3,2},{4,7},{5,4},{6,5},{7,6},{8,11},{9,8},{10,9... | collective-permute-start | bytes 2359304 | tf_op jit(solution)/shard_map/ppermute | solution.py:19
  73.7 8.3 %collective-permute-done.1 = bf16[768,512]{1,0:T(8,128)(2,1)} collective-permute-done((bf16[768,512]{1,0:T(8,128)(2,1)}, bf16[768,512]{1,0:T(8,128)(2,1)}, u32[]{:S(2)}, u32[]{:S(2)}) %collective-permute-start.1) | collective-permute-done | bytes 786464 | tf_op jit(solution)/shard_map/ppermute | solution.py:19
  83.9 2.7 %collective-permute-start.2 = (bf16[768,512]{1,0:T(8,128)(2,1)}, bf16[768,512]{1,0:T(8,128)(2,1)S(1)}, u32[]{:S(2)}, u32[]{:S(2)}) collective-permute-start(bf16[768,512]{1,0:T(8,128)(2,1)} %collective-permute-done), channel_id=1, source_target_pairs={{0,28},{4,0},{8,4},{12,8},{16,12},{20,16},{24,20},{28,24},{1,29},{... | collective-permute-start | bytes 2359304 | tf_op jit(solution)/shard_map/ppermute | solution.py:19
  95.0 26.8 %collective-permute-done.8 = bf16[1536,256]{1,0:T(8,128)(2,1)S(1)} collective-permute-done((bf16[1536,256]{1,0:T(8,128)(2,1)}, bf16[1536,256]{1,0:T(8,128)(2,1)S(1)}, u32[]{:S(2)}, u32[]{:S(2)}) %collective-permute-start.8) | collective-permute-done | bytes 786464 | tf_op jit(solution)/shard_map/ppermute | solution.py:19
  124.6 2.7 %collective-permute-start.4 = (bf16[768,512]{1,0:T(8,128)(2,1)S(1)}, bf16[768,512]{1,0:T(8,128)(2,1)S(1)}, u32[]{:S(2)}, u32[]{:S(2)}) collective-permute-start(bf16[768,512]{1,0:T(8,128)(2,1)S(1)} %collective-permute-done.2), channel_id=1, source_target_pairs={{0,28},{4,0},{8,4},{12,8},{16,12},{20,16},{24,20},{28,24},{1,29},{... | collective-permute-start | bytes 2359304 | tf_op jit(solution)/shard_map/ppermute | solution.py:19
  134.2 6.2 %collective-permute-done.4 = bf16[768,512]{1,0:T(8,128)(2,1)S(1)} collective-permute-done((bf16[768,512]{1,0:T(8,128)(2,1)S(1)}, bf16[768,512]{1,0:T(8,128)(2,1)S(1)}, u32[]{:S(2)}, u32[]{:S(2)}) %collective-permute-start.4) | collective-permute-done | bytes 786464 | tf_op jit(solution)/shard_map/ppermute | solution.py:19
  140.4 3.5 %collective-permute-start.7 = (bf16[384,512]{1,0:T(8,128)(2,1)S(1)}, bf16[384,512]{1,0:T(8,128)(2,1)S(1)}, u32[]{:S(2)}, u32[]{:S(2)}) collective-permute-start(bf16[384,512]{1,0:T(8,128)(2,1)S(1)} %slice.200), channel_id=1, source_target_pairs={{0,28},{4,0},{8,4},{12,8},{16,12},{20,16},{24,20},{28,24},{1,29},{... | collective-permute-start | bytes 1179656 | tf_op jit(solution)/shard_map/ppermute | solution.py:19
  145.6 3.3 %collective-permute-done.7 = bf16[384,512]{1,0:T(8,128)(2,1)S(1)} collective-permute-done((bf16[384,512]{1,0:T(8,128)(2,1)S(1)}, bf16[384,512]{1,0:T(8,128)(2,1)S(1)}, u32[]{:S(2)}, u32[]{:S(2)}) %collective-permute-start.7) | collective-permute-done | bytes 393248 | tf_op jit(solution)/shard_map/ppermute | solution.py:19
  154.8 4.2 %all-to-all-start.5 = ((bf16[4,256,256]{2,1,0:T(8,128)(2,1)}), bf16[4,256,256]{2,1,0:T(8,128)(2,1)}, u32[]{:S(2)}, u32[]{:S(2)}) async-start(bf16[4,256,256]{2,1,0:T(8,128)(2,1)} %broadcast_in_dim.73), calls=%async_computation.5 | async-start | bytes 1048576 | tf_op jit(solution)/shard_map/all_to_all | solution.py:117
  162.7 3.2 %all-to-all-done.5.hidden_ref = bf16[4,256,256]{2,1,0:T(8,128)(2,1)} async-done(((bf16[4,256,256]{2,1,0:T(8,128)(2,1)}), bf16[4,256,256]{2,1,0:T(8,128)(2,1)}, u32[]{:S(2)}, u32[]{:S(2)}) %all-to-all-start.5) | async-done | bytes 524320 | tf_op jit(solution)/shard_map/all_to_all | solution.py:117
  167.0 3.5 %all-to-all-start.3 = ((bf16[4,512,256]{2,1,0:T(8,128)(2,1)}), bf16[4,512,256]{2,1,0:T(8,128)(2,1)S(1)}, u32[]{:S(2)}, u32[]{:S(2)}) async-start(bf16[4,512,256]{2,1,0:T(8,128)(2,1)} %broadcast_in_dim.71), calls=%async_computation.3 | async-start | bytes 2097152 | tf_op jit(solution)/shard_map/all_to_all | solution.py:117
  170.5 6.9 %down_parts.4 = bf16[8,192,256]{2,1,0:T(8,128)(2,1)} custom-call(bf16[4,8,192,256]{3,2,1,0:T(8,128)(2,1)} %copy-done.1, bf16[4,256,256]{2,1,0:T(8,128)(2,1)} %all-to-all-done.5.hidden_ref), custom_call_target="tpu_custom_call" | custom-call | tf_op jit(solution)/shard_map/down_parts/pallas_call | solution.py:75
  181.2 4.2 %down_parts.5 = bf16[3,192,512]{2,1,0:T(8,128)(2,1)} custom-call(bf16[4,8,192,256]{3,2,1,0:T(8,128)(2,1)} %copy-done.1, bf16[4,512,256]{2,1,0:T(8,128)(2,1)} %copy-done.4), custom_call_target="tpu_custom_call" | custom-call | tf_op jit(solution)/shard_map/down_parts/pallas_call | solution.py:75
  186.7 2.7 %collective-permute-start.16 = (bf16[96,768]{1,0:T(8,128)(2,1)S(1)}, bf16[96,768]{1,0:T(8,128)(2,1)S(1)}, u32[]{:S(2)}, u32[]{:S(2)}) collective-permute-start(bf16[96,768]{1,0:T(8,128)(2,1)S(1)} %get-tuple-element.22), channel_id=1, source_target_pairs={{0,28},{4,0},{8,4},{12,8},{16,12},{20,16},{24,20},{28,24},{1,29},{... | collective-permute-start | bytes 442376 | tf_op jit(solution)/shard_map/ppermute | solution.py:19
  189.3 5.7 %down_parts.3 = bf16[5,192,512]{2,1,0:T(8,128)(2,1)} custom-call(bf16[4,8,192,256]{3,2,1,0:T(8,128)(2,1)} %copy-done.1, bf16[4,512,256]{2,1,0:T(8,128)(2,1)} %copy-done.4), custom_call_target="tpu_custom_call" | custom-call | tf_op jit(solution)/shard_map/down_parts/pallas_call | solution.py:75
  195.3 2.7 %collective-permute-start.17 = (bf16[192,768]{1,0:T(8,128)(2,1)S(1)}, bf16[192,768]{1,0:T(8,128)(2,1)S(1)}, u32[]{:S(2)}, u32[]{:S(2)}) collective-permute-start(bf16[192,768]{1,0:T(8,128)(2,1)S(1)} %pad_maximum_fusion), channel_id=1, source_target_pairs={{0,28},{4,0},{8,4},{12,8},{16,12},{20,16},{24,20},{28,24},{1,29},{... | collective-permute-start | bytes 884744 | tf_op jit(solution)/shard_map/ppermute | solution.py:19
  198.1 5.4 %collective-permute-done.13 = bf16[192,768]{1,0:T(8,128)(2,1)S(1)} collective-permute-done((bf16[192,768]{1,0:T(8,128)(2,1)S(1)}, bf16[192,768]{1,0:T(8,128)(2,1)S(1)}, u32[]{:S(2)}, u32[]{:S(2)}) %collective-permute-start.13) | collective-permute-done | bytes 294944 | tf_op jit(solution)/shard_map/ppermute | solution.py:19
  203.9 2.7 %collective-permute-start.18 = (bf16[192,768]{1,0:T(8,128)(2,1)S(1)}, bf16[192,768]{1,0:T(8,128)(2,1)S(1)}, u32[]{:S(2)}, u32[]{:S(2)}) collective-permute-start(bf16[192,768]{1,0:T(8,128)(2,1)S(1)} %add_convert_fusion.2), channel_id=1, source_target_pairs={{0,28},{4,0},{8,4},{12,8},{16,12},{20,16},{24,20},{28,24},{1,29},{... | collective-permute-start | bytes 884744 | tf_op jit(solution)/shard_map/ppermute | solution.py:19
  206.6 6.1 %collective-permute-done.14 = bf16[192,768]{1,0:T(8,128)(2,1)S(1)} collective-permute-done((bf16[192,768]{1,0:T(8,128)(2,1)S(1)}, bf16[192,768]{1,0:T(8,128)(2,1)S(1)}, u32[]{:S(2)}, u32[]{:S(2)}) %collective-permute-start.14) | collective-permute-done | bytes 294944 | tf_op jit(solution)/shard_map/ppermute | solution.py:19
  213.0 2.7 %collective-permute-start.19 = (bf16[192,768]{1,0:T(8,128)(2,1)S(1)}, bf16[192,768]{1,0:T(8,128)(2,1)S(1)}, u32[]{:S(2)}, u32[]{:S(2)}) collective-permute-start(bf16[192,768]{1,0:T(8,128)(2,1)S(1)} %add_convert_fusion.1), channel_id=1, source_target_pairs={{0,28},{4,0},{8,4},{12,8},{16,12},{20,16},{24,20},{28,24},{1,29},{... | collective-permute-start | bytes 884744 | tf_op jit(solution)/shard_map/ppermute | solution.py:19
  215.7 5.2 %collective-permute-done.15 = bf16[192,768]{1,0:T(8,128)(2,1)S(1)} collective-permute-done((bf16[192,768]{1,0:T(8,128)(2,1)S(1)}, bf16[192,768]{1,0:T(8,128)(2,1)S(1)}, u32[]{:S(2)}, u32[]{:S(2)}) %collective-permute-start.15) | collective-permute-done | bytes 294944 | tf_op jit(solution)/shard_map/ppermute | solution.py:19
  222.3 14.5 %all-to-all-start.6 = ((bf16[8,192,96]{2,1,0:T(8,128)(2,1)}), bf16[8,192,96]{2,1,0:T(8,128)(2,1)S(1)}, u32[]{:S(2)}, u32[]{:S(2)}) async-start(bf16[8,192,96]{2,1,0:T(8,128)(2,1)} %bitcast.193), calls=%async_computation.6 | async-start | bytes 786432 | tf_op jit(solution)/shard_map/all_to_all | solution.py:202
  236.9 7.7 %all-to-all-done.6 = bf16[8,192,96]{2,1,0:T(8,128)(2,1)S(1)} async-done(((bf16[8,192,96]{2,1,0:T(8,128)(2,1)}), bf16[8,192,96]{2,1,0:T(8,128)(2,1)S(1)}, u32[]{:S(2)}, u32[]{:S(2)}) %all-to-all-start.6) | async-done | bytes 294944 | tf_op jit(solution)/shard_map/all_to_all | solution.py:202
  (122 shorter events, 55.4 us)
Async XLA Ops:
  16.9 30.8 %copy-start.5 = (bf16[1,6144,256]{2,1,0:T(8,128)(2,1)S(1)}, bf16[1,6144,256]{2,1,0:T(8,128)(2,1)}, u32[]{:S(2)}) copy-start(bf16[1,6144,256]{2,1,0:T(8,128)(2,1)} %param.9) | copy-start | bytes 9437188
  19.4 15.6 %all-to-all-start.2 = ((bf16[4,192,512]{2,1,0:T(8,128)(2,1)}), bf16[4,192,512]{2,1,0:T(8,128)(2,1)}, u32[]{:S(2)}, u32[]{:S(2)}) async-start(bf16[4,192,512]{2,1,0:T(8,128)(2,1)} %broadcast_in_dim.70), calls=%async_computation.2 | async-start | bytes 1572864 | tf_op jit(solution)/shard_map/all_to_all | solution.py:117
  36.8 30.5 %all-to-all-start.4 = ((bf16[8,192,256]{2,1,0:T(8,128)(2,1)}), bf16[8,192,256]{2,1,0:T(8,128)(2,1)}, u32[]{:S(2)}, u32[]{:S(2)}) async-start(bf16[8,192,256]{2,1,0:T(8,128)(2,1)} %broadcast_in_dim.72), calls=%async_computation.4 | async-start | bytes 1572864 | tf_op jit(solution)/shard_map/all_to_all | solution.py:117
  45.0 36.9 %collective-permute-start.1 = (bf16[768,512]{1,0:T(8,128)(2,1)}, bf16[768,512]{1,0:T(8,128)(2,1)}, u32[]{:S(2)}, u32[]{:S(2)}) collective-permute-start(bf16[768,512]{1,0:T(8,128)(2,1)} %bitcast.10), channel_id=1, source_target_pairs={{0,4},{4,8},{8,12},{12,16},{16,20},{20,24},{24,28},{28,0},{1,5},{5... | collective-permute-start | bytes 2359304 | tf_op jit(solution)/shard_map/ppermute | solution.py:19
  46.5 37.4 %collective-permute-start = (bf16[768,512]{1,0:T(8,128)(2,1)}, bf16[768,512]{1,0:T(8,128)(2,1)}, u32[]{:S(2)}, u32[]{:S(2)}) collective-permute-start(bf16[768,512]{1,0:T(8,128)(2,1)} %bitcast.10), channel_id=1, source_target_pairs={{0,28},{4,0},{8,4},{12,8},{16,12},{20,16},{24,20},{28,24},{1,29},{... | collective-permute-start | bytes 2359304 | tf_op jit(solution)/shard_map/ppermute | solution.py:19
  67.3 86.5 %all-to-all-start = ((bf16[4,8,192,256]{3,2,1,0:T(8,128)(2,1)}), bf16[4,8,192,256]{3,2,1,0:T(8,128)(2,1)S(1)}, u32[]{:S(2)}, u32[]{:S(2)}) async-start(bf16[4,8,192,256]{3,2,1,0:T(8,128)(2,1)} %relayout_down.1), calls=%async_computation | async-start | bytes 6291456 | tf_op jit(solution)/shard_map/all_to_all | solution.py:161
  71.1 17.4 %copy-start.11 = (f32[512,256]{1,0:T(8,128)S(1)}, f32[512,256]{1,0:T(8,128)}, u32[]{:S(2)}) copy-start(f32[512,256]{1,0:T(8,128)} %fusion.44) | copy-start | bytes 1572868
  71.1 50.7 %collective-permute-start.8 = (bf16[1536,256]{1,0:T(8,128)(2,1)}, bf16[1536,256]{1,0:T(8,128)(2,1)S(1)}, u32[]{:S(2)}, u32[]{:S(2)}) collective-permute-start(bf16[1536,256]{1,0:T(8,128)(2,1)} %bitcast.32), channel_id=1, source_target_pairs={{0,3},{1,0},{2,1},{3,2},{4,7},{5,4},{6,5},{7,6},{8,11},{9,8},{10,9... | collective-permute-start | bytes 2359304 | tf_op jit(solution)/shard_map/ppermute | solution.py:19
  73.7 49.7 %collective-permute-start.9 = (bf16[1536,256]{1,0:T(8,128)(2,1)}, bf16[1536,256]{1,0:T(8,128)(2,1)S(1)}, u32[]{:S(2)}, u32[]{:S(2)}) collective-permute-start(bf16[1536,256]{1,0:T(8,128)(2,1)} %bitcast.32), channel_id=1, source_target_pairs={{0,1},{1,2},{2,3},{3,0},{4,5},{5,6},{6,7},{7,4},{8,9},{9,10},{10,1... | collective-permute-start | bytes 2359304 | tf_op jit(solution)/shard_map/ppermute | solution.py:19
  82.0 41.7 %collective-permute-start.3 = (bf16[768,512]{1,0:T(8,128)(2,1)}, bf16[768,512]{1,0:T(8,128)(2,1)S(1)}, u32[]{:S(2)}, u32[]{:S(2)}) collective-permute-start(bf16[768,512]{1,0:T(8,128)(2,1)} %collective-permute-done.1), channel_id=1, source_target_pairs={{0,4},{4,8},{8,12},{12,16},{16,20},{20,24},{24,28},{28,0},{1,5},{5... | collective-permute-start | bytes 2359304 | tf_op jit(solution)/shard_map/ppermute | solution.py:19
  82.0 8.3 %copy-start.6 = (bf16[1,6144,256]{2,1,0:T(8,128)(2,1)S(1)}, bf16[1,6144,256]{2,1,0:T(8,128)(2,1)}, u32[]{:S(2)}) copy-start(bf16[1,6144,256]{2,1,0:T(8,128)(2,1)} %param.9) | copy-start | bytes 9437188
  83.9 40.7 %collective-permute-start.2 = (bf16[768,512]{1,0:T(8,128)(2,1)}, bf16[768,512]{1,0:T(8,128)(2,1)S(1)}, u32[]{:S(2)}, u32[]{:S(2)}) collective-permute-start(bf16[768,512]{1,0:T(8,128)(2,1)} %collective-permute-done), channel_id=1, source_target_pairs={{0,28},{4,0},{8,4},{12,8},{16,12},{20,16},{24,20},{28,24},{1,29},{... | collective-permute-start | bytes 2359304 | tf_op jit(solution)/shard_map/ppermute | solution.py:19
  121.8 8.0 %collective-permute-start.11 = (bf16[768,256]{1,0:T(8,128)(2,1)S(1)}, bf16[768,256]{1,0:T(8,128)(2,1)S(1)}, u32[]{:S(2)}, u32[]{:S(2)}) collective-permute-start(bf16[768,256]{1,0:T(8,128)(2,1)S(1)} %slice.204), channel_id=1, source_target_pairs={{0,3},{1,0},{2,1},{3,2},{4,7},{5,4},{6,5},{7,6},{8,11},{9,8},{10,9... | collective-permute-start | bytes 1179656 | tf_op jit(solution)/shard_map/ppermute | solution.py:19
  123.4 9.0 %collective-permute-start.10 = (bf16[768,256]{1,0:T(8,128)(2,1)S(1)}, bf16[768,256]{1,0:T(8,128)(2,1)S(1)}, u32[]{:S(2)}, u32[]{:S(2)}) collective-permute-start(bf16[768,256]{1,0:T(8,128)(2,1)S(1)} %slice.203), channel_id=1, source_target_pairs={{0,1},{1,2},{2,3},{3,0},{4,5},{5,6},{6,7},{7,4},{8,9},{9,10},{10,1... | collective-permute-start | bytes 1179656 | tf_op jit(solution)/shard_map/ppermute | solution.py:19
  123.7 20.2 %collective-permute-start.5 = (bf16[768,512]{1,0:T(8,128)(2,1)S(1)}, bf16[768,512]{1,0:T(8,128)(2,1)S(1)}, u32[]{:S(2)}, u32[]{:S(2)}) collective-permute-start(bf16[768,512]{1,0:T(8,128)(2,1)S(1)} %collective-permute-done.3), channel_id=1, source_target_pairs={{0,4},{4,8},{8,12},{12,16},{16,20},{20,24},{24,28},{28,0},{1,5},{5... | collective-permute-start | bytes 2359304 | tf_op jit(solution)/shard_map/ppermute | solution.py:19
  124.6 15.7 %collective-permute-start.4 = (bf16[768,512]{1,0:T(8,128)(2,1)S(1)}, bf16[768,512]{1,0:T(8,128)(2,1)S(1)}, u32[]{:S(2)}, u32[]{:S(2)}) collective-permute-start(bf16[768,512]{1,0:T(8,128)(2,1)S(1)} %collective-permute-done.2), channel_id=1, source_target_pairs={{0,28},{4,0},{8,4},{12,8},{16,12},{20,16},{24,20},{28,24},{1,29},{... | collective-permute-start | bytes 2359304 | tf_op jit(solution)/shard_map/ppermute | solution.py:19
  140.3 11.8 %copy-start.9 = (bf16[768,512]{1,0:T(8,128)(2,1)}, bf16[768,512]{1,0:T(8,128)(2,1)S(1)}, u32[]{:S(2)}) copy-start(bf16[768,512]{1,0:T(8,128)(2,1)S(1)} %collective-permute-done.4) | copy-start | bytes 2359300
  140.4 8.5 %collective-permute-start.7 = (bf16[384,512]{1,0:T(8,128)(2,1)S(1)}, bf16[384,512]{1,0:T(8,128)(2,1)S(1)}, u32[]{:S(2)}, u32[]{:S(2)}) collective-permute-start(bf16[384,512]{1,0:T(8,128)(2,1)S(1)} %slice.200), channel_id=1, source_target_pairs={{0,28},{4,0},{8,4},{12,8},{16,12},{20,16},{24,20},{28,24},{1,29},{... | collective-permute-start | bytes 1179656 | tf_op jit(solution)/shard_map/ppermute | solution.py:19
  143.9 7.9 %collective-permute-start.6 = (bf16[384,512]{1,0:T(8,128)(2,1)S(1)}, bf16[384,512]{1,0:T(8,128)(2,1)S(1)}, u32[]{:S(2)}, u32[]{:S(2)}) collective-permute-start(bf16[384,512]{1,0:T(8,128)(2,1)S(1)} %slice.199), channel_id=1, source_target_pairs={{0,4},{4,8},{8,12},{12,16},{16,20},{20,24},{24,28},{28,0},{1,5},{5... | collective-permute-start | bytes 1179656 | tf_op jit(solution)/shard_map/ppermute | solution.py:19
  153.9 8.8 %copy-start.1 = (bf16[4,8,192,256]{3,2,1,0:T(8,128)(2,1)}, bf16[4,8,192,256]{3,2,1,0:T(8,128)(2,1)S(1)}, u32[]{:S(2)}) copy-start(bf16[4,8,192,256]{3,2,1,0:T(8,128)(2,1)S(1)} %all-to-all-done.down_ref) | copy-start | bytes 9437188
  154.8 11.2 %all-to-all-start.5 = ((bf16[4,256,256]{2,1,0:T(8,128)(2,1)}), bf16[4,256,256]{2,1,0:T(8,128)(2,1)}, u32[]{:S(2)}, u32[]{:S(2)}) async-start(bf16[4,256,256]{2,1,0:T(8,128)(2,1)} %broadcast_in_dim.73), calls=%async_computation.5 | async-start | bytes 1048576 | tf_op jit(solution)/shard_map/all_to_all | solution.py:117
  167.0 13.2 %all-to-all-start.3 = ((bf16[4,512,256]{2,1,0:T(8,128)(2,1)}), bf16[4,512,256]{2,1,0:T(8,128)(2,1)S(1)}, u32[]{:S(2)}, u32[]{:S(2)}) async-start(bf16[4,512,256]{2,1,0:T(8,128)(2,1)} %broadcast_in_dim.71), calls=%async_computation.3 | async-start | bytes 2097152 | tf_op jit(solution)/shard_map/all_to_all | solution.py:117
  186.6 8.5 %collective-permute-start.12 = (bf16[96,768]{1,0:T(8,128)(2,1)S(1)}, bf16[96,768]{1,0:T(8,128)(2,1)S(1)}, u32[]{:S(2)}, u32[]{:S(2)}) collective-permute-start(bf16[96,768]{1,0:T(8,128)(2,1)S(1)} %get-tuple-element.21), channel_id=1, source_target_pairs={{0,4},{4,8},{8,12},{12,16},{16,20},{20,24},{24,28},{28,0},{1,5},{5... | collective-permute-start | bytes 442376 | tf_op jit(solution)/shard_map/ppermute | solution.py:19
  186.7 8.6 %collective-permute-start.16 = (bf16[96,768]{1,0:T(8,128)(2,1)S(1)}, bf16[96,768]{1,0:T(8,128)(2,1)S(1)}, u32[]{:S(2)}, u32[]{:S(2)}) collective-permute-start(bf16[96,768]{1,0:T(8,128)(2,1)S(1)} %get-tuple-element.22), channel_id=1, source_target_pairs={{0,28},{4,0},{8,4},{12,8},{16,12},{20,16},{24,20},{28,24},{1,29},{... | collective-permute-start | bytes 442376 | tf_op jit(solution)/shard_map/ppermute | solution.py:19
  195.1 8.4 %collective-permute-start.13 = (bf16[192,768]{1,0:T(8,128)(2,1)S(1)}, bf16[192,768]{1,0:T(8,128)(2,1)S(1)}, u32[]{:S(2)}, u32[]{:S(2)}) collective-permute-start(bf16[192,768]{1,0:T(8,128)(2,1)S(1)} %fusion.77), channel_id=1, source_target_pairs={{0,4},{4,8},{8,12},{12,16},{16,20},{20,24},{24,28},{28,0},{1,5},{5... | collective-permute-start | bytes 884744 | tf_op jit(solution)/shard_map/ppermute | solution.py:19
  195.3 8.4 %collective-permute-start.17 = (bf16[192,768]{1,0:T(8,128)(2,1)S(1)}, bf16[192,768]{1,0:T(8,128)(2,1)S(1)}, u32[]{:S(2)}, u32[]{:S(2)}) collective-permute-start(bf16[192,768]{1,0:T(8,128)(2,1)S(1)} %pad_maximum_fusion), channel_id=1, source_target_pairs={{0,28},{4,0},{8,4},{12,8},{16,12},{20,16},{24,20},{28,24},{1,29},{... | collective-permute-start | bytes 884744 | tf_op jit(solution)/shard_map/ppermute | solution.py:19
  203.7 33.2 %copy-start.12 = (f32[256,2]{0,1:T(2,128)S(1)}, f32[256,2]{0,1:T(2,128)}, u32[]{:S(2)}) copy-start(f32[256,2]{0,1:T(2,128)} %param.8) | copy-start | bytes 6148
  203.7 9.0 %collective-permute-start.14 = (bf16[192,768]{1,0:T(8,128)(2,1)S(1)}, bf16[192,768]{1,0:T(8,128)(2,1)S(1)}, u32[]{:S(2)}, u32[]{:S(2)}) collective-permute-start(bf16[192,768]{1,0:T(8,128)(2,1)S(1)} %add_convert_fusion.4), channel_id=1, source_target_pairs={{0,4},{4,8},{8,12},{12,16},{16,20},{20,24},{24,28},{28,0},{1,5},{5... | collective-permute-start | bytes 884744 | tf_op jit(solution)/shard_map/ppermute | solution.py:19
  203.9 9.0 %collective-permute-start.18 = (bf16[192,768]{1,0:T(8,128)(2,1)S(1)}, bf16[192,768]{1,0:T(8,128)(2,1)S(1)}, u32[]{:S(2)}, u32[]{:S(2)}) collective-permute-start(bf16[192,768]{1,0:T(8,128)(2,1)S(1)} %add_convert_fusion.2), channel_id=1, source_target_pairs={{0,28},{4,0},{8,4},{12,8},{16,12},{20,16},{24,20},{28,24},{1,29},{... | collective-permute-start | bytes 884744 | tf_op jit(solution)/shard_map/ppermute | solution.py:19
  212.8 8.2 %collective-permute-start.15 = (bf16[192,768]{1,0:T(8,128)(2,1)S(1)}, bf16[192,768]{1,0:T(8,128)(2,1)S(1)}, u32[]{:S(2)}, u32[]{:S(2)}) collective-permute-start(bf16[192,768]{1,0:T(8,128)(2,1)S(1)} %add_convert_fusion.3), channel_id=1, source_target_pairs={{0,4},{4,8},{8,12},{12,16},{16,20},{20,24},{24,28},{28,0},{1,5},{5... | collective-permute-start | bytes 884744 | tf_op jit(solution)/shard_map/ppermute | solution.py:19
  213.0 8.0 %collective-permute-start.19 = (bf16[192,768]{1,0:T(8,128)(2,1)S(1)}, bf16[192,768]{1,0:T(8,128)(2,1)S(1)}, u32[]{:S(2)}, u32[]{:S(2)}) collective-permute-start(bf16[192,768]{1,0:T(8,128)(2,1)S(1)} %add_convert_fusion.1), channel_id=1, source_target_pairs={{0,28},{4,0},{8,4},{12,8},{16,12},{20,16},{24,20},{28,24},{1,29},{... | collective-permute-start | bytes 884744 | tf_op jit(solution)/shard_map/ppermute | solution.py:19
  222.3 22.2 %all-to-all-start.6 = ((bf16[8,192,96]{2,1,0:T(8,128)(2,1)}), bf16[8,192,96]{2,1,0:T(8,128)(2,1)S(1)}, u32[]{:S(2)}, u32[]{:S(2)}) async-start(bf16[8,192,96]{2,1,0:T(8,128)(2,1)} %bitcast.193), calls=%async_computation.6 | async-start | bytes 786432 | tf_op jit(solution)/shard_map/all_to_all | solution.py:202
  (7 other events, 23.3 us)
